TPU v7x, 32 devices: a whole 2x2x4 slice. The times are simulated.
32 devices in a mesh: groups: 2 (over y), cells: 4 (over z), corners: 2 (over x), kern: 2 (over core).
Axes of the slice: x: 2, y: 2, z: 4, core: 2. Of those that a mesh axis runs over, the one named last changes fastest.
Arguments:
- theta: float32 [64, 128, 128], P(('groups', 'cells')), parts along dimension 0, may hold values from -8 to 8
- target: bfloat16 [16, 128, 128], P(('groups', 'cells')), parts along dimension 0, may hold values from 0 to 1
- kernels: float32 [2, 2, 24, 35, 35], P(None, 'corners', 'kern'), may hold values from -25.33743 to 25.33743
- dose: float32 [2], P('corners'), may hold values from 0.6 to 1
- inst_owner: int32 [128, 1], P(('groups', 'cells')), parts along dimension 0, may hold values from 0 to 3; in each aligned block of 16 rows (0 to 15, 16 to 31, ...) at most 8 rows name the same one
- inst_local: int32 [128], P(('groups', 'cells')), parts along dimension 0, may hold values from 0 to 7
- inst_shift: int32 [128], P(('groups', 'cells')), parts along dimension 0, may hold values from 0 to 127
Outputs:
- theta_out: float32 [64, 128, 128], P(('groups', 'cells'), ('corners', 'kern')), parts along dimension 0
There are 2 independent parts, one for each index of `groups`. A program takes and returns all parts, laid end to end along the dimension named above; an argument that names none is the same for every part. Nothing has to cross between parts.
Inputs may be any that keep to these rules, and one draw needn't show every extreme that they name: `inst_owner`: within the rows of one device (aligned blocks of 16 rows) no owner is named by more than 8 rows, and in some block one owner is named by exactly 8.
All inputs are finite; a program needn't handle non-finite values.
Results may differ from a plain program's by a relative error of at most 0.003.
Values may be sent and summed in bfloat16 or wider, within the bound.
No kernel may reach another device: no remote copies, remote signals or barrier semaphores. Data moves between devices by JAX's collectives and lax.ppermute only.
A program may use at most 64 MiB of HBM per device.

v0:
```python
import functools

import jax
import jax.numpy as jnp
import numpy as np
from jax import lax
from jax.experimental import pallas as pl
from jax.experimental.pallas import tpu as pltpu
from jax.sharding import PartitionSpec as P


ITERS = 2
LR = 0.25
EPS = 1e-06
STEEP = 3.0
LANES = 128
HALF = LANES // 2
INFO = 16
BF = jnp.bfloat16
F32 = jnp.float32


def up(value, step):
    return -(-value // step) * step


def split(array):
    high = np.asarray(array, np.float32).astype(BF)
    low = (np.asarray(array, np.float32) - high.astype(np.float32)).astype(BF)
    return high, low


class Tables:
    def __init__(self, cell, freq):
        self.cell, self.freq = cell, freq
        self.mid = freq // 2
        self.rows = up(self.mid + 1, 8)
        self.grid = min(cell, up(4 * self.mid + 1, 8))
        rows, grid, mid = self.rows, self.grid, self.mid
        turn = 2.0 * np.pi / cell
        f = np.arange(mid + 1)
        g = np.arange(freq) - mid
        pixels = np.arange(cell)
        fy = np.zeros((cell, LANES))
        phase = (pixels[:, None] * g[None, :] % cell) * turn
        fy[:, :freq] = np.cos(phase)
        fy[:, HALF : HALF + freq] = -np.sin(phase)
        self.fy = np.concatenate(split(fy), axis=1)
        fx = np.zeros((2 * rows, cell))
        phase = (f[:, None] * pixels[None, :] % cell) * turn
        fx[: mid + 1] = np.cos(phase)
        fx[rows : rows + mid + 1] = np.sin(phase)
        self.fx = np.concatenate(split(fx), axis=0)
        ex = np.concatenate([fx[:rows].T, -fx[rows:].T], axis=1)
        self.ex = ex.astype(np.float32)
        gy = np.zeros((LANES, 2 * cell))
        phase = (g[:, None] * pixels[None, :] % cell) * turn
        gy[:freq, :cell] = np.cos(phase)
        gy[:freq, cell:] = np.sin(phase)
        gy[HALF : HALF + freq, :cell] = -np.sin(phase)
        gy[HALF : HALF + freq, cell:] = np.cos(phase)
        self.gy = gy.astype(np.float32)
        both = np.concatenate([gy, np.roll(gy, HALF, axis=0)], axis=0)
        self.gyy = both.astype(np.float32).astype(BF)
        self.gyy_t = self.gyy.T.copy()
        gx = np.zeros((2 * grid, 4 * rows))
        phase = (f[None, :] * np.arange(grid)[:, None] % grid) * (2.0 * np.pi / grid)
        cos, sin = np.zeros((grid, rows)), np.zeros((grid, rows))
        cos[:, : mid + 1], sin[:, : mid + 1] = np.cos(phase), np.sin(phase)
        gx[:grid] = np.concatenate([cos, cos, -sin, -sin], axis=1)
        gx[grid:] = np.concatenate([sin, -sin, cos, -cos], axis=1)
        self.gx = gx.astype(np.float32).astype(BF)
        self.gx_t = self.gx.T.copy()
        u = np.arange(-2 * mid, 2 * mid + 1)
        if grid == cell:
            weights = np.eye(cell)
        else:
            diff = pixels[:, None] / cell - np.arange(grid)[None, :] / grid
            weights = np.cos(2.0 * np.pi * diff[:, :, None] * u).sum(-1) / grid
        self.w = weights.astype(np.float32)
        self.w_t = self.w.T.copy()
        ph = np.zeros((cell, 2 * LANES))
        phase = (pixels[:, None] * g[None, :] % cell) * turn
        ph[:, :freq] = ph[:, HALF : HALF + freq] = np.cos(phase)
        ph[:, LANES : LANES + freq] = np.sin(phase)
        ph[:, LANES + HALF : LANES + HALF + freq] = -np.sin(phase)
        self.ph = ph.astype(np.float32)
        self.ph_split = np.concatenate(split(ph), axis=1)
        pick_u, pick_v = np.zeros((rows, freq)), np.zeros((rows, freq))
        for row in range(mid + 1):
            pick_u[row, mid + row] = 1.0
            if row > 0:
                pick_v[row, mid - row] = 1.0
        self.pick = np.stack([pick_u, pick_v]).astype(np.float32).astype(BF)
        lane = np.zeros((4, freq, LANES))
        for col in range(freq):
            lane[0, col, col] = 1.0
            lane[1, col, HALF + col] = 1.0
            lane[2, col, freq - 1 - col] = 1.0
            lane[3, col, HALF + freq - 1 - col] = -1.0
        self.lane = lane.astype(np.float32).astype(BF)


def packing(tabs):
    sent = tabs.rows - 8
    free = HALF - tabs.freq
    extra = tabs.mid + 1 - sent
    pieces = -(-tabs.freq // free) if free > 0 else 0
    if sent % 16 or free < 8 or extra < 1 or extra * pieces > 8:
        return up(tabs.rows, 16), []
    steps = []
    for p in range(pieces):
        begin = p * free
        steps.append((begin, min(free, tabs.freq - begin), p * extra, extra))
    return sent, steps


def inside(first, count, value):
    return (value >= first) & (value < first + count)


def pack(tabs, spec):
    sent, steps = packing(tabs)
    if not steps:
        return jnp.concatenate([spec, jnp.zeros((sent - tabs.rows, LANES), F32)], axis=0).astype(BF)
    row = lax.broadcasted_iota(jnp.int32, (8, LANES), 0)
    col = lane_of((8, LANES)) % HALF
    top, rest = spec[:8], spec[sent:]
    for begin, width, where, extra in steps:
        moved = pltpu.roll(rest, tabs.freq - begin, 1)
        if where:
            moved = pltpu.roll(moved, where, 0)
        here = inside(where, extra, row) & inside(tabs.freq, width, col)
        top = jnp.where(here, moved, top)
    return jnp.concatenate([top, spec[8:sent]], axis=0).astype(BF)


def unpack(tabs, sent_spec):
    _, steps = packing(tabs)
    if not steps:
        return sent_spec[: tabs.rows].astype(F32)
    spec = sent_spec.astype(F32)
    row = lax.broadcasted_iota(jnp.int32, (8, LANES), 0)
    col = lane_of((8, LANES)) % HALF
    rest = jnp.zeros((8, LANES), F32)
    for begin, width, where, extra in steps:
        moved = pltpu.roll(spec[:8], LANES - (tabs.freq - begin), 1)
        if where:
            moved = pltpu.roll(moved, 8 - where, 0)
        here = inside(0, extra, row) & inside(begin, width, col)
        rest = jnp.where(here, moved, rest)
    return jnp.concatenate([spec, rest], axis=0)


def dot(a, b, **kw):
    return jnp.dot(a, b, preferred_element_type=F32, **kw)


def exact(a, b):
    return dot(a, b, precision=lax.Precision.HIGHEST)


def swap(x):
    return pltpu.roll(x, HALF, 1)


def lane_of(shape):
    return lax.broadcasted_iota(jnp.int32, shape, len(shape) - 1)


def arrange_body(dose, kern, pick, lane, out):
    root = jnp.sqrt(jnp.full((1, 1), dose[0], F32))
    for k in range(out.shape[0]):
        real = (kern[0, 0, k] * root).astype(BF)
        imag = (kern[1, 0, k] * root).astype(BF)
        upper = (dot(real, lane[0]) + dot(imag, lane[1])).astype(BF)
        lower = (dot(real, lane[2]) + dot(imag, lane[3])).astype(BF)
        both = jnp.concatenate([dot(pick[0], upper), dot(pick[1], lower)], axis=0)
        out[k] = both.astype(BF)


def spectra(tabs, slots, theta, fy, fx, out):
    cells, cell, rows = theta.shape[0], tabs.cell, tabs.rows
    mask = jax.nn.sigmoid(theta).astype(BF).reshape(cells * cell, cell)
    along = dot(mask, fy[...])
    along = along[:, :LANES] + along[:, LANES:]
    sign = jnp.where(lane_of((rows, LANES)) < HALF, 1.0, -1.0)
    row_at = lax.broadcasted_iota(jnp.int32, (rows, LANES), 0)
    centre = jnp.where((row_at == 0) & (lane_of((rows, LANES)) == tabs.mid), 1.0 / slots, 0.0)
    scale = 2.0 / (slots * cell * cell)
    for c in range(cells):
        part = along[c * cell : (c + 1) * cell]
        high = part.astype(BF)
        low = (part - high.astype(F32)).astype(BF)
        res = dot(fx[...], jnp.concatenate([high, low], axis=1))
        res = res[: 2 * rows, :LANES] + res[: 2 * rows, LANES:] + res[2 * rows :, :LANES]
        spec = res[:rows] + swap(res[rows:]) * sign
        sent = packing(tabs)[0]
        out[c * sent : (c + 1) * sent] = pack(tabs, spec * scale - centre)


def first_body(tabs, slots, owner, local, shift, theta, fy, fx, out):
    spectra(tabs, slots, theta[...], fy, fx, out)
    base = theta.shape[0] * packing(tabs)[0]
    row = lax.broadcasted_iota(jnp.int32, (INFO, LANES), 0)
    col = lane_of((INFO, LANES))
    info = jnp.zeros((INFO, LANES), jnp.int32)
    for i in range(local.shape[0]):
        value = jnp.where(row == 0, owner[i], jnp.where(row == 1, local[i], shift[i]))
        info = jnp.where((col == i) & (row < 3), value, info)
    out[base : base + INFO] = info.astype(F32).astype(BF)


def counts(tabs, n, tiles, cells, slots, at, ph, payload, out):
    z = at[0]
    base = cells * packing(tabs)[0]
    row = lax.broadcasted_iota(jnp.int32, (tiles * cells, LANES), 0)
    col = lane_of((tiles * cells, LANES))
    shift_at = lax.broadcasted_iota(jnp.int32, (tabs.cell, LANES), 0)
    for k in range(n):
        info = payload[k][base : base + INFO].astype(F32).astype(jnp.int32)
        owner, local, shift = info[0:1], info[1:2], info[2:3]
        mine = (owner == z) & (local == row % cells) & (col // slots == row // cells)
        mine = mine & (col < tiles * slots)
        chosen = jnp.where(mine, 1.0, 0.0).astype(BF)
        hot = jnp.where(shift == shift_at, 1.0, 0.0).astype(BF)
        number = lax.dot_general(
            chosen, hot, (((1,), (1,)), ((), ())), preferred_element_type=F32
        ).astype(BF)
        sums = dot(number, ph[...])
        sums = sums[:, : 2 * LANES] + sums[:, 2 * LANES :]
        source = lax.rem(z - k + n, n)
        out[pl.ds(source * tiles, tiles)] = sums.reshape(tiles, cells, 2 * LANES)


def tile_body(tabs, n, cells, tiles, copies, at, owner, local, shift, *refs):
    payload, refs = refs[:n], refs[n:]
    arranged, refs = refs[:tiles], refs[tiles:]
    target, ph, gyy, gyy_t, gx, gx_t, w, w_t, out, held, near = refs
    rows, cell, grid = tabs.rows, tabs.cell, tabs.grid
    slots = local.shape[0] // tiles
    z, j = at[0], at[1]
    for k in range(n):
        sent = packing(tabs)[0]
        held[pl.ds(k * cells, cells)] = payload[k][0 : cells * sent].reshape(cells, sent, LANES)
    spec = jnp.zeros((rows, LANES), F32)
    for s in range(slots):
        i = j * slots + s
        which = lax.rem(z - owner[i] + n, n) * cells + local[i]
        one = unpack(tabs, held[which])
        turn = ph[pl.ds(shift[i], 1)]
        spec = spec + one * turn[:, :LANES] + swap(one) * turn[:, LANES:]
    left = lane_of((rows, LANES)) < HALF
    other = swap(spec)
    real = jnp.where(left, spec, other)
    imag = jnp.where(left, other, -spec)
    real = jnp.concatenate([real, real], axis=0)
    imag = jnp.concatenate([imag, imag], axis=0)
    wanted = target[j].astype(F32)
    sum_real = jnp.zeros((2 * rows, LANES), F32)
    sum_imag = jnp.zeros((2 * rows, LANES), F32)
    span = 2 * rows
    members = [(ref, k) for ref in arranged for k in range(ref.shape[0])]
    pairs = [members[m : m + 2] for m in range(0, len(members), 2)]
    total = jnp.zeros((grid, 2 * cell), F32)
    for number, pair in enumerate(pairs):
        wide = []
        for ref, k in pair:
            kern = ref[k].astype(F32)
            wide.append(
                jnp.concatenate([(kern * real).astype(BF), (kern * imag).astype(BF)], axis=1)
            )
        rowed = dot(jnp.concatenate(wide, axis=0), gyy[...])
        cols = [
            jnp.concatenate(
                [rowed[p * span : (p + 1) * span, :cell], rowed[p * span : (p + 1) * span, cell:]],
                axis=0,
            )
            for p in range(len(pair))
        ]
        fields = dot(gx[...], jnp.concatenate(cols, axis=1).astype(BF))
        near[number] = fields
        total = total + fields[:grid] * fields[:grid] + fields[grid:] * fields[grid:]
    image = exact(w[...], total[:, :cell] + total[:, cell:])
    resist = jax.nn.sigmoid(STEEP * (image - 1.0))
    pressure = 4.0 * STEEP * (resist - wanted) * resist * (1.0 - resist)
    push = exact(w_t[...], pressure)
    push = jnp.concatenate([push, push], axis=0)
    push = jnp.concatenate([push, push], axis=1)
    for number, pair in enumerate(pairs):
        back = dot(gx_t[...], (near[number] * push).astype(BF)).astype(BF)
        rowed = jnp.concatenate(
            [
                jnp.concatenate(
                    [back[:span, p * cell : (p + 1) * cell], back[span:, p * cell : (p + 1) * cell]],
                    axis=1,
                )
                for p in range(len(pair))
            ],
            axis=0,
        )
        wide = dot(rowed, gyy_t[...])
        for p, (ref, k) in enumerate(pair):
            kern = ref[k].astype(F32)
            sum_real = sum_real + kern * wide[p * span : (p + 1) * span, :LANES]
            sum_imag = sum_imag + kern * wide[p * span : (p + 1) * span, LANES:]
    sum_real = sum_real[:rows] + sum_real[rows:]
    sum_imag = sum_imag[:rows] + sum_imag[rows:]
    grad = jnp.where(left, sum_real + swap(sum_real), swap(sum_imag - swap(sum_imag)))
    grad = pack(tabs, grad)
    for copy in range(copies):
        out[copy] = grad


def gradients(tabs, slots, corners, kern, theta, grads, sums, gy, ex):
    tiles, cells = sums.shape[0], theta.shape[0]
    rows, cell = tabs.rows, tabs.cell
    pieces = []
    own = []
    for t in range(tiles):
        z, j = t // kern, t % kern
        parts = [unpack(tabs, grads[(z * corners + x) * kern + j]) for x in range(corners)]
        own.append(sum(parts[1:], parts[0]))
    swapped = [swap(grad) for grad in own]
    for c in range(cells):
        total = jnp.zeros((rows, LANES), F32)
        for t in range(tiles):
            turn = sums[t, c : c + 1]
            total = total + own[t] * turn[:, :LANES] - swapped[t] * turn[:, LANES:]
        pieces.append(total * (2.0 / (slots * cell * cell)))
    rowed = exact(jnp.concatenate(pieces, axis=0), gy[...])
    result = []
    for c in range(cells):
        part = rowed[c * rows : (c + 1) * rows]
        part = jnp.concatenate([part[:, :cell], part[:, cell:]], axis=0)
        squash = jax.nn.sigmoid(theta[c])
        gradient = exact(ex[...], part) * squash * (1.0 - squash)
        power = jnp.sum(jnp.sum(gradient * gradient, axis=0, keepdims=True), axis=1, keepdims=True)
        result.append((gradient, LR * lax.rsqrt(power / (cell * cell) + EPS)))
    return result


def update_body(tabs, slots, corners, kern, n, at, theta, grads, ph, gy, ex, fy, fx, *refs):
    heard, (out, sums, payload) = refs[:n], refs[n:]
    counts(tabs, n, kern, theta.shape[0], slots, at, ph, heard, sums)
    for c, (gradient, rate) in enumerate(
        gradients(tabs, slots, corners, kern, theta, grads, sums, gy, ex)
    ):
        out[c] = theta[c] - rate * gradient
    spectra(tabs, slots, out[...], fy, fx, payload)


def last_body(tabs, slots, corners, kern, at, theta, grads, sums, gy, ex, out, held, ready, sem):
    band = out.shape[1]
    start = pl.multiple_of(at[2] * band, band)
    copies = []
    for c, (gradient, rate) in enumerate(
        gradients(tabs, slots, corners, kern, theta, grads, sums, gy, ex)
    ):
        held[c] = rate * gradient
        ready[c] = theta[c, pl.ds(start, band)] - held[c, pl.ds(start, band)]
        copies.append(pltpu.make_async_copy(ready.at[c], out.at[c], sem.at[c]))
        copies[-1].start()
    for copy in copies:
        copy.wait()


VMEM = pl.BlockSpec(memory_space=pltpu.VMEM)
SMEM = pl.BlockSpec(memory_space=pltpu.SMEM)


def call(body, scalars, arrays, outs, scratch=(), far=(), out_far=False):
    many = isinstance(outs, list)
    arrays = [
        array if place in far else pltpu.with_memory_space_constraint(array, pltpu.VMEM)
        for place, array in enumerate(arrays)
    ]
    out_spec = pl.BlockSpec(memory_space=pl.ANY) if out_far else VMEM
    return pl.pallas_call(
        body,
        out_shape=outs,
        in_specs=[SMEM] * len(scalars) + [VMEM] * len(arrays),
        out_specs=[VMEM] * len(outs) if many else out_spec,
        scratch_shapes=list(scratch),
    )(*scalars, *arrays)


def shape(dims, dtype):
    return pltpu.VMEM(dims, dtype)


def shifted(array, axis, step):
    n = lax.axis_size(axis)
    return lax.ppermute(array, axis, [(i, (i + step) % n) for i in range(n)])


def per_device(theta, target, kernels, dose, inst_owner, inst_local, inst_shift):
    n = lax.axis_size("cells")
    n_kern = lax.axis_size("kern")
    n_corners = lax.axis_size("corners")
    cells, cell = theta.shape[0], theta.shape[1]
    tiles = target.shape[0]
    slots = inst_local.shape[0] // tiles
    assert tiles == n_kern
    tabs = Tables(cell, kernels.shape[3])
    inst_owner = inst_owner[:, 0]
    rows, sent = tabs.rows, packing(tabs)[0]
    at = jnp.stack(
        [lax.axis_index("cells"), lax.axis_index("kern"), lax.axis_index(("corners", "kern"))]
    ).astype(jnp.int32)
    band = cell // (n_kern * n_corners)
    payload = call(
        functools.partial(first_body, tabs, slots),
        [inst_owner, inst_local, inst_shift],
        [theta, tabs.fy, tabs.fx],
        shape((cells * sent + INFO, LANES), BF),
        far=(0, 1, 2),
    )
    payloads = [payload]
    for k in range(1, n):
        payloads.append(shifted(payload, "cells", k))
    own = call(
        arrange_body,
        [dose],
        [kernels, tabs.pick, tabs.lane],
        shape((kernels.shape[2], 2 * rows, LANES), BF),
    )
    arranged = [own] + [shifted(own, "kern", k) for k in range(1, n_kern)]
    copies = n * n_corners * n_kern
    for iteration in range(ITERS):
        grads = call(
            functools.partial(tile_body, tabs, n, cells, tiles, copies),
            [at, inst_owner, inst_local, inst_shift],
            payloads
            + arranged
            + [target, tabs.ph, tabs.gyy, tabs.gyy_t, tabs.gx, tabs.gx_t, tabs.w, tabs.w_t],
            shape((copies, sent, LANES), BF),
            scratch=[
                pltpu.VMEM((n * cells, sent, LANES), BF),
                pltpu.VMEM(
                    ((n_kern * kernels.shape[2] + 1) // 2, 2 * tabs.grid, 2 * cell), F32
                ),
            ],
        )
        grads = lax.all_to_all(grads, ("cells", "corners", "kern"), 0, 0, tiled=True)
        if iteration == ITERS - 1:
            return call(
                functools.partial(last_body, tabs, slots, n_corners, n_kern),
                [at],
                [theta, grads, sums, tabs.gy, tabs.ex],
                jax.ShapeDtypeStruct((cells, band, cell), F32),
                scratch=[
                    pltpu.VMEM((cells, cell, cell), F32),
                    pltpu.VMEM((cells, band, cell), F32),
                    pltpu.SemaphoreType.DMA((cells,)),
                ],
                out_far=True,
            )
        theta, sums, payload = call(
            functools.partial(update_body, tabs, slots, n_corners, n_kern, n),
            [at],
            [theta, grads, tabs.ph_split, tabs.gy, tabs.ex, tabs.fy, tabs.fx] + payloads,
            [
                shape(theta.shape, F32),
                shape((n * tiles, cells, 2 * LANES), F32),
                shape((cells * sent, LANES), BF),
            ],
        )
        payloads = [payload] + [shifted(payload, "cells", k) for k in range(1, n)]


def solution(mesh):
    in_specs = (
        P(("groups", "cells"), None, None),
        P(("groups", "cells"), None, None),
        P(None, "corners", "kern", None, None),
        P("corners"),
        P(("groups", "cells"), None),
        P(("groups", "cells")),
        P(("groups", "cells")),
    )
    out_specs = P(("groups", "cells"), ("corners", "kern"), None)
    return jax.shard_map(
        per_device, mesh=mesh, in_specs=in_specs, out_specs=out_specs, check_vma=False
    )
```

profile of v0, /device:TPU:0, one launch (start us, length us, event | category | flops | bytes accessed | tf_op | source)
XLA Modules:
  0.0 57.8 jit_solution(11664147858174304694)
XLA Ops:
  0.7 0.0 copy-start.14
  0.7 0.0 copy-start.15
  0.7 1.1 %copy.22.kern = f32[2,1,12,35,35]{4,3,2,1,0:T(8,128)S(1)} copy(f32[2,1,12,35,35]{4,1,3,2,0:T(1,128)} %param.23) | data formatting | bytes 235200 | tf_op args[2]
  1.8 1.9 %shard_map.200.refs_4_ = bf16[12,48,128]{2,1,0:T(8,128)(2,1)S(1)} custom-call(f32[1]{0:T(128)S(6)} %copy.23.dose, f32[2,1,12,35,35]{4,3,2,1,0:T(8,128)S(1)} %copy.22.kern, bf16[2,24,35]{2,1,0:T(8,128)(2,1)S(1)} %copy-done.15, bf16[4,35,128]{2,1,0:T(8,128)(2,1)S(1)} %copy-done.14), custom_call_target="tpu_custom_call" | custom-call | tf_op jit(solution)/shard_map/pallas_call | solution.py:379
  3.7 0.5 collective-permute-start.3
  4.2 0.0 copy-start.7
  4.2 0.0 copy-start.9
  4.2 0.0 copy-start.10
  4.3 1.9 %shard_map.199.refs_0_ = bf16[144,128]{1,0:T(8,128)(2,1)S(1)} custom-call(s32[16]{0:T(128)} %bitcast.4, s32[16]{0:T(128)} %local.5, s32[16]{0:T(128)} %shift.5, f32[8,128,128]{2,1,0:T(8,128)} %theta.3, bf16[128,256]{1,0:T(8,128)(2,1)} %constant.41.clone.fy, bf16[96,128]{1,0:T(8,128)(2,1)} %constant.42.clone.fx), custom_call_target="tpu_custom_call" | custom-call | tf_op jit(solution)/shard_map/pallas_call | solution.py:379
  6.1 4.6 %collective-permute-start.2 = (bf16[144,128]{1,0:T(8,128)(2,1)S(1)}, bf16[144,128]{1,0:T(8,128)(2,1)S(1)}, u32[]{:S(2)}, u32[]{:S(2)}) collective-permute-start(bf16[144,128]{1,0:T(8,128)(2,1)S(1)} %shard_map.199.refs_0_), channel_id=1, source_target_pairs={{0,12},{4,0},{8,4},{12,8},{1,13},{5,1},{9,5},{13,9},{2,14},{6,2},{... | collective-permute-start | bytes 110600 | tf_op jit(solution)/shard_map/ppermute | solution.py:394
  10.8 1.0 %collective-permute-start = (bf16[144,128]{1,0:T(8,128)(2,1)S(1)}, bf16[144,128]{1,0:T(8,128)(2,1)S(1)}, u32[]{:S(2)}, u32[]{:S(2)}) collective-permute-start(bf16[144,128]{1,0:T(8,128)(2,1)S(1)} %shard_map.199.refs_0_), channel_id=1, source_target_pairs={{0,4},{4,8},{8,12},{12,0},{1,5},{5,9},{9,13},{13,1},{2,6},{6,10},{... | collective-permute-start | bytes 110600 | tf_op jit(solution)/shard_map/ppermute | solution.py:394
  11.8 0.7 %pad_add_fusion.at = s32[3]{0:T(128)} fusion(s32[1]{0:T(128)} %bitcast.2, s32[1]{0:T(128)} %bitcast.1, s32[1]{0:T(128)} %bitcast), kind=kLoop, calls=%fused_computation | loop fusion | flops 6 | bytes 24 | tf_op jit(solution)/shard_map/stack | solution.py:408
  12.5 0.2 collective-permute-done.2.refs_3_
  12.6 3.4 %collective-permute-done.1.refs_2_ = bf16[144,128]{1,0:T(8,128)(2,1)S(1)} collective-permute-done((bf16[144,128]{1,0:T(8,128)(2,1)S(1)}, bf16[144,128]{1,0:T(8,128)(2,1)S(1)}, u32[]{:S(2)}, u32[]{:S(2)}) %collective-permute-start.1) | collective-permute-done | bytes 36896 | tf_op jit(solution)/shard_map/ppermute | solution.py:394
  16.0 0.5 collective-permute-done.refs_1_
  16.6 0.0 copy-start.6
  16.6 0.0 copy-start.8
  16.6 0.0 copy-start.12
  16.6 0.0 copy-start.13
  16.7 4.2 %shard_map.201 = bf16[16,16,128]{2,1,0:T(8,128)(2,1)S(1)} custom-call(s32[3]{0:T(128)} %pad_add_fusion.at, s32[16]{0:T(128)} %bitcast.5, s32[16]{0:T(128)} %local.5, s32[16]{0:T(128)} %shift.5, bf16[144,128]{1,0:T(8,128)(2,1)S(1)} %shard_map.199.refs_0_, bf16[144,128]{1,0:T(8,128)(2,1)S(1)} %collective-permute-done.refs_1_, ...), custom_call_target="tpu_custom_call" | custom-call | tf_op jit(solution)/shard_map/pallas_call | solution.py:379
  20.9 0.0 copy-start.4
  20.9 10.4 %all_to_all.10.grads = bf16[16,16,128]{2,1,0:T(8,128)(2,1)S(1)} all-to-all(bf16[16,16,128]{2,1,0:T(8,128)(2,1)S(1)} %shard_map.201), channel_id=1, replica_groups=mesh['groups'=2,'cells'=4,'corners'=2,'kern'=2] {'cells','corners','kern'}, dimensions={0} | all-to-all | bytes 131072 | tf_op jit(solution)/shard_map/all_to_all | solution.py:445
  31.3 2.9 %shard_map.202 = (f32[8,128,128]{2,1,0:T(8,128)S(1)}, f32[8,8,256]{2,1,0:T(8,128)S(1)}, bf16[128,128]{1,0:T(8,128)(2,1)S(1)}) custom-call(s32[3]{0:T(128)} %pad_add_fusion.at, f32[8,128,128]{2,1,0:T(8,128)S(1)} %copy-done, bf16[16,16,128]{2,1,0:T(8,128)(2,1)S(1)} %all_to_all.10.grads, bf16[128,512]{1,0:T(8,128)(2,1)S(1)} %copy-done.12, ...), custom_call_target="tpu_custom_call" | custom-call | tf_op jit(solution)/shard_map/pallas_call | solution.py:379
  34.2 0.6 collective-permute-start.6
  34.8 1.0 %collective-permute-start.5 = (bf16[128,128]{1,0:T(8,128)(2,1)S(1)}, bf16[128,128]{1,0:T(8,128)(2,1)S(1)}, u32[]{:S(2)}, u32[]{:S(2)}) collective-permute-start(bf16[128,128]{1,0:T(8,128)(2,1)S(1)} %get-tuple-element.9.refs_0_), channel_id=1, source_target_pairs={{0,8},{4,12},{8,0},{12,4},{1,9},{5,13},{9,1},{13,5},{2,10},{6,14},... | collective-permute-start | bytes 98312 | tf_op jit(solution)/shard_map/ppermute | solution.py:394
  35.8 0.7 %collective-permute-start.4 = (bf16[128,128]{1,0:T(8,128)(2,1)S(1)}, bf16[128,128]{1,0:T(8,128)(2,1)S(1)}, u32[]{:S(2)}, u32[]{:S(2)}) collective-permute-start(bf16[128,128]{1,0:T(8,128)(2,1)S(1)} %get-tuple-element.9.refs_0_), channel_id=1, source_target_pairs={{0,4},{4,8},{8,12},{12,0},{1,5},{5,9},{9,13},{13,1},{2,6},{6,10},{... | collective-permute-start | bytes 98312 | tf_op jit(solution)/shard_map/ppermute | solution.py:394
  36.5 1.7 %collective-permute-done.6.refs_3_ = bf16[128,128]{1,0:T(8,128)(2,1)S(1)} collective-permute-done((bf16[128,128]{1,0:T(8,128)(2,1)S(1)}, bf16[128,128]{1,0:T(8,128)(2,1)S(1)}, u32[]{:S(2)}, u32[]{:S(2)}) %collective-permute-start.6) | collective-permute-done | bytes 32800 | tf_op jit(solution)/shard_map/ppermute | solution.py:394
  38.2 1.4 %collective-permute-done.5.refs_2_ = bf16[128,128]{1,0:T(8,128)(2,1)S(1)} collective-permute-done((bf16[128,128]{1,0:T(8,128)(2,1)S(1)}, bf16[128,128]{1,0:T(8,128)(2,1)S(1)}, u32[]{:S(2)}, u32[]{:S(2)}) %collective-permute-start.5) | collective-permute-done | bytes 32800 | tf_op jit(solution)/shard_map/ppermute | solution.py:394
  39.6 1.9 %collective-permute-done.4.refs_1_ = bf16[128,128]{1,0:T(8,128)(2,1)S(1)} collective-permute-done((bf16[128,128]{1,0:T(8,128)(2,1)S(1)}, bf16[128,128]{1,0:T(8,128)(2,1)S(1)}, u32[]{:S(2)}, u32[]{:S(2)}) %collective-permute-start.4) | collective-permute-done | bytes 32800 | tf_op jit(solution)/shard_map/ppermute | solution.py:394
  41.6 4.1 %shard_map.203 = bf16[16,16,128]{2,1,0:T(8,128)(2,1)S(1)} custom-call(s32[3]{0:T(128)} %pad_add_fusion.at, s32[16]{0:T(128)} %bitcast.6, s32[16]{0:T(128)} %local.5, s32[16]{0:T(128)} %shift.5, bf16[128,128]{1,0:T(8,128)(2,1)S(1)} %get-tuple-element.9.refs_0_, bf16[128,128]{1,0:T(8,128)(2,1)S(1)} %collective-permute-done.4.refs_1_, ...), custom_call_target="tpu_custom_call" | custom-call | tf_op jit(solution)/shard_map/pallas_call | solution.py:379
  45.6 9.5 %all_to_all.11.grads = bf16[16,16,128]{2,1,0:T(8,128)(2,1)S(1)} all-to-all(bf16[16,16,128]{2,1,0:T(8,128)(2,1)S(1)} %shard_map.203), channel_id=1, replica_groups=mesh['groups'=2,'cells'=4,'corners'=2,'kern'=2] {'cells','corners','kern'}, dimensions={0} | all-to-all | bytes 131072 | tf_op jit(solution)/shard_map/all_to_all | solution.py:445
  55.1 2.7 %shard_map.204 = f32[8,32,128]{2,1,0:T(8,128)} custom-call(s32[3]{0:T(128)} %pad_add_fusion.at, f32[8,128,128]{2,1,0:T(8,128)S(1)} %get-tuple-element.8.theta, bf16[16,16,128]{2,1,0:T(8,128)(2,1)S(1)} %all_to_all.11.grads, f32[8,8,256]{2,1,0:T(8,128)S(1)} %get-tuple-element.10.sums, f32[128,256]{1,0:T(8,128)S(1)} %copy-done.4, f32[128,48]{1,0:T(8,128)S(1)} %copy-done.6), custom_call_target="tpu_custom_call" | custom-call | tf_op jit(solution)/shard_map/pallas_call | solution.py:379
  (24 shorter events, 0.1 us)
Async XLA Ops:
  0.7 1.1 %copy-start.14 = (bf16[4,35,128]{2,1,0:T(8,128)(2,1)S(1)}, bf16[4,35,128]{2,1,0:T(8,128)(2,1)}, u32[]{:S(2)}) copy-start(bf16[4,35,128]{2,1,0:T(8,128)(2,1)} %constant.44.clone.lane) | copy-start | bytes 107524
  0.7 1.1 %copy-start.15 = (bf16[2,24,35]{2,1,0:T(8,128)(2,1)S(1)}, bf16[2,24,35]{2,1,0:T(8,128)(2,1)}, u32[]{:S(2)}) copy-start(bf16[2,24,35]{2,1,0:T(8,128)(2,1)} %constant.43.clone.pick) | copy-start | bytes 10084
  3.7 12.8 %collective-permute-start.3 = (bf16[12,48,128]{2,1,0:T(8,128)(2,1)S(1)}, bf16[12,48,128]{2,1,0:T(8,128)(2,1)S(1)}, u32[]{:S(2)}, u32[]{:S(2)}) collective-permute-start(bf16[12,48,128]{2,1,0:T(8,128)(2,1)S(1)} %shard_map.200.refs_4_), channel_id=1, source_target_pairs={{0,1},{1,0},{2,3},{3,2},{4,5},{5,4},{6,7},{7,6},{8,9},{9,8},{10,11... | collective-permute-start | bytes 442376 | tf_op jit(solution)/shard_map/ppermute | solution.py:394
  4.2 12.3 %copy-start.1 = (bf16[256,256]{1,0:T(8,128)(2,1)S(1)}, bf16[256,256]{1,0:T(8,128)(2,1)}, u32[]{:S(2)}) copy-start(bf16[256,256]{1,0:T(8,128)(2,1)} %constant.47.clone.refs_9_) | copy-start | bytes 393220
  4.2 12.3 %copy-start.2 = (bf16[256,256]{1,0:T(8,128)(2,1)S(1)}, bf16[256,256]{1,0:T(8,128)(2,1)}, u32[]{:S(2)}) copy-start(bf16[256,256]{1,0:T(8,128)(2,1)} %constant.46.clone.refs_8_) | copy-start | bytes 393220
  4.2 12.3 %copy-start.3 = (f32[128,256]{1,0:T(8,128)S(1)}, f32[128,256]{1,0:T(8,128)}, u32[]{:S(2)}) copy-start(f32[128,256]{1,0:T(8,128)} %constant.45.clone.refs_7_) | copy-start | bytes 393220
  4.2 12.4 %copy-start.5 = (bf16[2,128,128]{2,1,0:T(8,128)(2,1)S(1)}, bf16[2,128,128]{2,1,0:T(8,128)(2,1)}, u32[]{:S(2)}) copy-start(bf16[2,128,128]{2,1,0:T(8,128)(2,1)} %refs_6_.3) | copy-start | bytes 196612
  4.2 12.4 %copy-start.7 = (f32[128,72]{1,0:T(8,128)S(1)}, f32[128,72]{1,0:T(8,128)}, u32[]{:S(2)}) copy-start(f32[128,72]{1,0:T(8,128)} %constant.50.clone.refs_12_) | copy-start | bytes 110596
  4.2 12.4 %copy-start.9 = (bf16[96,144]{1,0:T(8,128)(2,1)S(1)}, bf16[96,144]{1,0:T(8,128)(2,1)}, u32[]{:S(2)}) copy-start(bf16[96,144]{1,0:T(8,128)(2,1)} %constant.49.clone.refs_11_) | copy-start | bytes 82948
  4.2 12.4 %copy-start.10 = (f32[72,128]{1,0:T(8,128)S(1)}, f32[72,128]{1,0:T(8,128)}, u32[]{:S(2)}) copy-start(f32[72,128]{1,0:T(8,128)} %constant.51.clone.refs_13_) | copy-start | bytes 110596
  4.2 12.4 %copy-start.11 = (bf16[144,96]{1,0:T(8,128)(2,1)S(1)}, bf16[144,96]{1,0:T(8,128)(2,1)}, u32[]{:S(2)}) copy-start(bf16[144,96]{1,0:T(8,128)(2,1)} %constant.48.clone.refs_10_) | copy-start | bytes 82948
  6.1 6.5 %collective-permute-start.2 = (bf16[144,128]{1,0:T(8,128)(2,1)S(1)}, bf16[144,128]{1,0:T(8,128)(2,1)S(1)}, u32[]{:S(2)}, u32[]{:S(2)}) collective-permute-start(bf16[144,128]{1,0:T(8,128)(2,1)S(1)} %shard_map.199.refs_0_), channel_id=1, source_target_pairs={{0,12},{4,0},{8,4},{12,8},{1,13},{5,1},{9,5},{13,9},{2,14},{6,2},{... | collective-permute-start | bytes 110600 | tf_op jit(solution)/shard_map/ppermute | solution.py:394
  10.8 5.3 %collective-permute-start.1 = (bf16[144,128]{1,0:T(8,128)(2,1)S(1)}, bf16[144,128]{1,0:T(8,128)(2,1)S(1)}, u32[]{:S(2)}, u32[]{:S(2)}) collective-permute-start(bf16[144,128]{1,0:T(8,128)(2,1)S(1)} %shard_map.199.refs_0_), channel_id=1, source_target_pairs={{0,8},{4,12},{8,0},{12,4},{1,9},{5,13},{9,1},{13,5},{2,10},{6,14},... | collective-permute-start | bytes 110600 | tf_op jit(solution)/shard_map/ppermute | solution.py:394
  10.8 5.8 %collective-permute-start = (bf16[144,128]{1,0:T(8,128)(2,1)S(1)}, bf16[144,128]{1,0:T(8,128)(2,1)S(1)}, u32[]{:S(2)}, u32[]{:S(2)}) collective-permute-start(bf16[144,128]{1,0:T(8,128)(2,1)S(1)} %shard_map.199.refs_0_), channel_id=1, source_target_pairs={{0,4},{4,8},{8,12},{12,0},{1,5},{5,9},{9,13},{13,1},{2,6},{6,10},{... | collective-permute-start | bytes 110600 | tf_op jit(solution)/shard_map/ppermute | solution.py:394
  12.5 18.8 %copy-start = (f32[8,128,128]{2,1,0:T(8,128)S(1)}, f32[8,128,128]{2,1,0:T(8,128)}, u32[]{:S(2)}) copy-start(f32[8,128,128]{2,1,0:T(8,128)} %theta.3) | copy-start | bytes 1572868
  16.6 14.7 %copy-start.6 = (f32[128,48]{1,0:T(8,128)S(1)}, f32[128,48]{1,0:T(8,128)}, u32[]{:S(2)}) copy-start(f32[128,48]{1,0:T(8,128)} %constant.54.clone.ex) | copy-start | bytes 73732
  16.6 14.7 %copy-start.8 = (bf16[128,256]{1,0:T(8,128)(2,1)S(1)}, bf16[128,256]{1,0:T(8,128)(2,1)}, u32[]{:S(2)}) copy-start(bf16[128,256]{1,0:T(8,128)(2,1)} %constant.41.clone.fy) | copy-start | bytes 196612
  16.6 14.7 %copy-start.12 = (bf16[128,512]{1,0:T(8,128)(2,1)S(1)}, bf16[128,512]{1,0:T(8,128)(2,1)}, u32[]{:S(2)}) copy-start(bf16[128,512]{1,0:T(8,128)(2,1)} %constant.52.clone.ph) | copy-start | bytes 393220
  16.6 14.7 %copy-start.13 = (bf16[96,128]{1,0:T(8,128)(2,1)S(1)}, bf16[96,128]{1,0:T(8,128)(2,1)}, u32[]{:S(2)}) copy-start(bf16[96,128]{1,0:T(8,128)(2,1)} %constant.42.clone.fx) | copy-start | bytes 73732
  20.9 10.5 %copy-start.4 = (f32[128,256]{1,0:T(8,128)S(1)}, f32[128,256]{1,0:T(8,128)}, u32[]{:S(2)}) copy-start(f32[128,256]{1,0:T(8,128)} %constant.53.clone.gy) | copy-start | bytes 393220
  34.2 3.9 %collective-permute-start.6 = (bf16[128,128]{1,0:T(8,128)(2,1)S(1)}, bf16[128,128]{1,0:T(8,128)(2,1)S(1)}, u32[]{:S(2)}, u32[]{:S(2)}) collective-permute-start(bf16[128,128]{1,0:T(8,128)(2,1)S(1)} %get-tuple-element.9.refs_0_), channel_id=1, source_target_pairs={{0,12},{4,0},{8,4},{12,8},{1,13},{5,1},{9,5},{13,9},{2,14},{6,2},{... | collective-permute-start | bytes 98312 | tf_op jit(solution)/shard_map/ppermute | solution.py:394
  34.8 4.8 %collective-permute-start.5 = (bf16[128,128]{1,0:T(8,128)(2,1)S(1)}, bf16[128,128]{1,0:T(8,128)(2,1)S(1)}, u32[]{:S(2)}, u32[]{:S(2)}) collective-permute-start(bf16[128,128]{1,0:T(8,128)(2,1)S(1)} %get-tuple-element.9.refs_0_), channel_id=1, source_target_pairs={{0,8},{4,12},{8,0},{12,4},{1,9},{5,13},{9,1},{13,5},{2,10},{6,14},... | collective-permute-start | bytes 98312 | tf_op jit(solution)/shard_map/ppermute | solution.py:394
  35.8 5.7 %collective-permute-start.4 = (bf16[128,128]{1,0:T(8,128)(2,1)S(1)}, bf16[128,128]{1,0:T(8,128)(2,1)S(1)}, u32[]{:S(2)}, u32[]{:S(2)}) collective-permute-start(bf16[128,128]{1,0:T(8,128)(2,1)S(1)} %get-tuple-element.9.refs_0_), channel_id=1, source_target_pairs={{0,4},{4,8},{8,12},{12,0},{1,5},{5,9},{9,13},{13,1},{2,6},{6,10},{... | collective-permute-start | bytes 98312 | tf_op jit(solution)/shard_map/ppermute | solution.py:394
where the time goes:
time: 58.1 us; the launch traced here: 57.8 us
  blocking collectives  19.9 us (34%)
  Pallas kernels  17.7 us (30%)
  waiting for transfers between devices  9.14 us (16%)
  starting transfers between devices  8.41 us (14%)
  local copies, waits for them, and re-layouts  1.15 us (2%)
  between operations  0.87 us (1%)
  other arithmetic  0.67 us (1%)
    all_to_all x2, blocking collectives, per_device(): lax.all_to_all(grads, ('cells', 'corners', 'kern'), 0, 0, tiled=True)  19.9 us
    pallas_call x6, Pallas kernels, call(): pl.pallas_call(body, out_shape=outs, in_specs=[SMEM] * len(scalars) + [VM...  17.7 us
    ppermute x7, waiting for transfers between devices, shifted(): return lax.ppermute(array, axis, [(i, (i + step) % n) for i in range(n)])  9.14 us
    ppermute x7, starting transfers between devices, shifted(): return lax.ppermute(array, axis, [(i, (i + step) % n) for i in range(n)])  8.41 us
  transfers between devices with their start and end apart: 7, of which 6 were waited for; matrix products, arithmetic and copies ran while one was open for 1% of the time, Pallas kernels for 3%

commit v1 on v0

--- a/solution.py
+++ b/solution.py
@@ -16,6 +16,7 @@
 LANES = 128
 HALF = LANES // 2
 INFO = 16
+CHUNK = 8
 BF = jnp.bfloat16
 F32 = jnp.float32
 
@@ -52,14 +53,14 @@
         fx[rows : rows + mid + 1] = np.sin(phase)
         self.fx = np.concatenate(split(fx), axis=0)
         ex = np.concatenate([fx[:rows].T, -fx[rows:].T], axis=1)
-        self.ex = ex.astype(np.float32)
+        self.ex = ex.astype(np.float32).astype(BF)
         gy = np.zeros((LANES, 2 * cell))
         phase = (g[:, None] * pixels[None, :] % cell) * turn
         gy[:freq, :cell] = np.cos(phase)
         gy[:freq, cell:] = np.sin(phase)
         gy[HALF : HALF + freq, :cell] = -np.sin(phase)
         gy[HALF : HALF + freq, cell:] = np.cos(phase)
-        self.gy = gy.astype(np.float32)
+        self.gy = gy.astype(np.float32).astype(BF)
         both = np.concatenate([gy, np.roll(gy, HALF, axis=0)], axis=0)
         self.gyy = both.astype(np.float32).astype(BF)
         self.gyy_t = self.gyy.T.copy()
@@ -77,8 +78,10 @@
         else:
             diff = pixels[:, None] / cell - np.arange(grid)[None, :] / grid
             weights = np.cos(2.0 * np.pi * diff[:, :, None] * u).sum(-1) / grid
-        self.w = weights.astype(np.float32)
-        self.w_t = self.w.T.copy()
+        high, low = split(weights)
+        self.w = np.zeros((cell, up(3 * grid, 16)), np.float32).astype(BF)
+        self.w[:, : 3 * grid] = np.concatenate([high, high, low], axis=1)
+        self.w_t = high.T.copy()
         ph = np.zeros((cell, 2 * LANES))
         phase = (pixels[:, None] * g[None, :] % cell) * turn
         ph[:, :freq] = ph[:, HALF : HALF + freq] = np.cos(phase)
@@ -156,10 +159,6 @@
     return jnp.dot(a, b, preferred_element_type=F32, **kw)
 
 
-def exact(a, b):
-    return dot(a, b, precision=lax.Precision.HIGHEST)
-
-
 def swap(x):
     return pltpu.roll(x, HALF, 1)
 
@@ -217,6 +216,7 @@
     row = lax.broadcasted_iota(jnp.int32, (tiles * cells, LANES), 0)
     col = lane_of((tiles * cells, LANES))
     shift_at = lax.broadcasted_iota(jnp.int32, (tabs.cell, LANES), 0)
+    numbers = []
     for k in range(n):
         info = payload[k][base : base + INFO].astype(F32).astype(jnp.int32)
         owner, local, shift = info[0:1], info[1:2], info[2:3]
@@ -224,19 +224,21 @@
         mine = mine & (col < tiles * slots)
         chosen = jnp.where(mine, 1.0, 0.0).astype(BF)
         hot = jnp.where(shift == shift_at, 1.0, 0.0).astype(BF)
-        number = lax.dot_general(
-            chosen, hot, (((1,), (1,)), ((), ())), preferred_element_type=F32
-        ).astype(BF)
-        sums = dot(number, ph[...])
-        sums = sums[:, : 2 * LANES] + sums[:, 2 * LANES :]
+        numbers.append(
+            lax.dot_general(chosen, hot, (((1,), (1,)), ((), ())), preferred_element_type=F32)
+        )
+    sums = dot(jnp.concatenate(numbers, axis=0).astype(BF), ph[...])
+    sums = sums[:, : 2 * LANES] + sums[:, 2 * LANES :]
+    for k in range(n):
         source = lax.rem(z - k + n, n)
-        out[pl.ds(source * tiles, tiles)] = sums.reshape(tiles, cells, 2 * LANES)
+        part = sums[k * tiles * cells : (k + 1) * tiles * cells]
+        out[pl.ds(source * tiles, tiles)] = part.reshape(tiles, cells, 2 * LANES)
 
 
 def tile_body(tabs, n, cells, tiles, copies, at, owner, local, shift, *refs):
     payload, refs = refs[:n], refs[n:]
     arranged, refs = refs[:tiles], refs[tiles:]
-    target, ph, gyy, gyy_t, gx, gx_t, w, w_t, out, held, near = refs
+    target, ph, gyy, gyy_t, gx, gx_t, w, w_t, out, held, wide, tall, near = refs
     rows, cell, grid = tabs.rows, tabs.cell, tabs.grid
     slots = local.shape[0] // tiles
     z, j = at[0], at[1]
@@ -257,53 +259,56 @@
     real = jnp.concatenate([real, real], axis=0)
     imag = jnp.concatenate([imag, imag], axis=0)
     wanted = target[j].astype(F32)
-    sum_real = jnp.zeros((2 * rows, LANES), F32)
-    sum_imag = jnp.zeros((2 * rows, LANES), F32)
     span = 2 * rows
     members = [(ref, k) for ref in arranged for k in range(ref.shape[0])]
-    pairs = [members[m : m + 2] for m in range(0, len(members), 2)]
-    total = jnp.zeros((grid, 2 * cell), F32)
-    for number, pair in enumerate(pairs):
-        wide = []
-        for ref, k in pair:
-            kern = ref[k].astype(F32)
-            wide.append(
-                jnp.concatenate([(kern * real).astype(BF), (kern * imag).astype(BF)], axis=1)
-            )
-        rowed = dot(jnp.concatenate(wide, axis=0), gyy[...])
-        cols = [
-            jnp.concatenate(
-                [rowed[p * span : (p + 1) * span, :cell], rowed[p * span : (p + 1) * span, cell:]],
-                axis=0,
-            )
-            for p in range(len(pair))
-        ]
-        fields = dot(gx[...], jnp.concatenate(cols, axis=1).astype(BF))
-        near[number] = fields
-        total = total + fields[:grid] * fields[:grid] + fields[grid:] * fields[grid:]
-    image = exact(w[...], total[:, :cell] + total[:, cell:])
+    number = len(members)
+    for m, (ref, k) in enumerate(members):
+        kern = ref[k].astype(F32)
+        wide[m * span : (m + 1) * span, :LANES] = (kern * real).astype(BF)
+        wide[m * span : (m + 1) * span, LANES:] = (kern * imag).astype(BF)
+    for first in range(0, number, CHUNK):
+        last = min(first + CHUNK, number)
+        res = dot(wide[first * span : last * span], gyy[...])
+        for m in range(first, last):
+            part = res[(m - first) * span : (m - first + 1) * span]
+            tall[m] = jnp.concatenate([part[:, :cell], part[:, cell:]], axis=0).astype(BF)
+    total = jnp.zeros((grid, cell), F32)
+    for m in range(0, number, 2):
+        pair = [tall[m + p] for p in range(min(2, number - m))]
+        fields = dot(gx[...], jnp.concatenate(pair, axis=1))
+        for p in range(len(pair)):
+            one = fields[:, p * cell : (p + 1) * cell]
+            near[m + p] = one
+            total = total + (one[:grid] * one[:grid] + one[grid:] * one[grid:])
+    high = total.astype(BF).astype(F32)
+    stack = [high, total - high, high]
+    if w.shape[1] > 3 * grid:
+        stack.append(jnp.zeros((w.shape[1] - 3 * grid, cell), F32))
+    image = dot(w[...], jnp.concatenate(stack, axis=0).astype(BF))
     resist = jax.nn.sigmoid(STEEP * (image - 1.0))
     pressure = 4.0 * STEEP * (resist - wanted) * resist * (1.0 - resist)
-    push = exact(w_t[...], pressure)
-    push = jnp.concatenate([push, push], axis=0)
-    push = jnp.concatenate([push, push], axis=1)
-    for number, pair in enumerate(pairs):
-        back = dot(gx_t[...], (near[number] * push).astype(BF)).astype(BF)
-        rowed = jnp.concatenate(
-            [
-                jnp.concatenate(
-                    [back[:span, p * cell : (p + 1) * cell], back[span:, p * cell : (p + 1) * cell]],
-                    axis=1,
-                )
-                for p in range(len(pair))
-            ],
-            axis=0,
-        )
-        wide = dot(rowed, gyy_t[...])
-        for p, (ref, k) in enumerate(pair):
+    push = dot(w_t[...], pressure.astype(BF))
+    for m in range(0, number, 2):
+        pair = []
+        for p in range(min(2, number - m)):
+            one = near[m + p]
+            pair.append(jnp.concatenate([one[:grid] * push, one[grid:] * push], axis=0))
+        back = dot(gx_t[...], jnp.concatenate(pair, axis=1).astype(BF)).astype(BF)
+        for p in range(len(pair)):
+            at_row = (m + p) * span
+            wide[at_row : at_row + span, :LANES] = back[:span, p * cell : (p + 1) * cell]
+            wide[at_row : at_row + span, LANES:] = back[span:, p * cell : (p + 1) * cell]
+    sum_real = jnp.zeros((span, LANES), F32)
+    sum_imag = jnp.zeros((span, LANES), F32)
+    for first in range(0, number, CHUNK):
+        last = min(first + CHUNK, number)
+        res = dot(wide[first * span : last * span], gyy_t[...])
+        for m in range(first, last):
+            ref, k = members[m]
             kern = ref[k].astype(F32)
-            sum_real = sum_real + kern * wide[p * span : (p + 1) * span, :LANES]
-            sum_imag = sum_imag + kern * wide[p * span : (p + 1) * span, LANES:]
+            part = res[(m - first) * span : (m - first + 1) * span]
+            sum_real = sum_real + kern * part[:, :LANES]
+            sum_imag = sum_imag + kern * part[:, LANES:]
     sum_real = sum_real[:rows] + sum_real[rows:]
     sum_imag = sum_imag[:rows] + sum_imag[rows:]
     grad = jnp.where(left, sum_real + swap(sum_real), swap(sum_imag - swap(sum_imag)))
@@ -319,8 +324,8 @@
     own = []
     for t in range(tiles):
         z, j = t // kern, t % kern
-        parts = [unpack(tabs, grads[(z * corners + x) * kern + j]) for x in range(corners)]
-        own.append(sum(parts[1:], parts[0]))
+        parts = [grads[(z * corners + x) * kern + j].astype(F32) for x in range(corners)]
+        own.append(unpack(tabs, sum(parts[1:], parts[0])))
     swapped = [swap(grad) for grad in own]
     for c in range(cells):
         total = jnp.zeros((rows, LANES), F32)
@@ -328,15 +333,20 @@
             turn = sums[t, c : c + 1]
             total = total + own[t] * turn[:, :LANES] - swapped[t] * turn[:, LANES:]
         pieces.append(total * (2.0 / (slots * cell * cell)))
-    rowed = exact(jnp.concatenate(pieces, axis=0), gy[...])
+    rowed = dot(jnp.concatenate(pieces, axis=0).astype(BF), gy[...])
     result = []
-    for c in range(cells):
-        part = rowed[c * rows : (c + 1) * rows]
-        part = jnp.concatenate([part[:, :cell], part[:, cell:]], axis=0)
-        squash = jax.nn.sigmoid(theta[c])
-        gradient = exact(ex[...], part) * squash * (1.0 - squash)
-        power = jnp.sum(jnp.sum(gradient * gradient, axis=0, keepdims=True), axis=1, keepdims=True)
-        result.append((gradient, LR * lax.rsqrt(power / (cell * cell) + EPS)))
+    for first in range(0, cells, 2):
+        columns = []
+        for c in range(first, min(first + 2, cells)):
+            part = rowed[c * rows : (c + 1) * rows]
+            columns.append(jnp.concatenate([part[:, :cell], part[:, cell:]], axis=0))
+        planes = dot(ex[...], jnp.concatenate(columns, axis=1).astype(BF))
+        for p in range(len(columns)):
+            squash = jax.nn.sigmoid(theta[first + p])
+            gradient = planes[:, p * cell : (p + 1) * cell] * squash * (1.0 - squash)
+            power = jnp.sum(gradient * gradient, axis=0, keepdims=True)
+            power = jnp.sum(power, axis=1, keepdims=True)
+            result.append((gradient, LR * lax.rsqrt(power / (cell * cell) + EPS)))
     return result
 
 
@@ -437,9 +447,9 @@
             shape((copies, sent, LANES), BF),
             scratch=[
                 pltpu.VMEM((n * cells, sent, LANES), BF),
-                pltpu.VMEM(
-                    ((n_kern * kernels.shape[2] + 1) // 2, 2 * tabs.grid, 2 * cell), F32
-                ),
+                pltpu.VMEM((n_kern * kernels.shape[2] * 2 * rows, 2 * LANES), BF),
+                pltpu.VMEM((n_kern * kernels.shape[2], 4 * rows, cell), BF),
+                pltpu.VMEM((n_kern * kernels.shape[2], 2 * tabs.grid, cell), F32),
             ],
         )
         grads = lax.all_to_all(grads, ("cells", "corners", "kern"), 0, 0, tiled=True)

time: 58.1 us -> 53.9 us (0.928)
  Pallas kernels: 17.7 us -> 13.5 us
    pallas_call x6, Pallas kernels: 17.7 us -> 13.5 us  [call(): pl.pallas_call(body, out_shape=outs, in_specs=[SMEM] * len(scalars) + [VM...]
where the time goes in v1:
time: 53.9 us; the launch traced here: 53.6 us
  blocking collectives  19.9 us (37%)
  Pallas kernels  13.5 us (25%)
  waiting for transfers between devices  9.14 us (17%)
  starting transfers between devices  8.44 us (16%)
  local copies, waits for them, and re-layouts  1.14 us (2%)
  between operations  0.86 us (2%)
  other arithmetic  0.67 us (1%)
    all_to_all x2, blocking collectives, per_device(): lax.all_to_all(grads, ('cells', 'corners', 'kern'), 0, 0, tiled=True)  19.9 us
    pallas_call x6, Pallas kernels, call(): pl.pallas_call(body, out_shape=outs, in_specs=[SMEM] * len(scalars) + [VM...  13.5 us
    ppermute x7, waiting for transfers between devices, shifted(): return lax.ppermute(array, axis, [(i, (i + step) % n) for i in range(n)])  9.14 us
    ppermute x7, starting transfers between devices, shifted(): return lax.ppermute(array, axis, [(i, (i + step) % n) for i in range(n)])  8.44 us
    unnamed x33, local copies, waits for them, and re-layouts  1.14 us
  transfers between devices with their start and end apart: 7, of which 6 were waited for; matrix products, arithmetic and copies ran while one was open for 1% of the time, Pallas kernels for 3%

profile of v1, /device:TPU:0, one launch (start us, length us, event | category | flops | bytes accessed | tf_op | source)
XLA Modules:
  0.0 53.6 jit_solution(7418692270516933062)
XLA Ops:
  0.7 0.0 copy-start.14
  0.7 0.0 copy-start.15
  0.7 1.1 %copy.22.kern = f32[2,1,12,35,35]{4,3,2,1,0:T(8,128)S(1)} copy(f32[2,1,12,35,35]{4,1,3,2,0:T(1,128)} %param.23) | data formatting | bytes 235200 | tf_op args[2]
  1.8 1.9 %shard_map.200.refs_4_ = bf16[12,48,128]{2,1,0:T(8,128)(2,1)S(1)} custom-call(f32[1]{0:T(128)S(6)} %copy.23.dose, f32[2,1,12,35,35]{4,3,2,1,0:T(8,128)S(1)} %copy.22.kern, bf16[2,24,35]{2,1,0:T(8,128)(2,1)S(1)} %copy-done.15, bf16[4,35,128]{2,1,0:T(8,128)(2,1)S(1)} %copy-done.14), custom_call_target="tpu_custom_call" | custom-call | tf_op jit(solution)/shard_map/pallas_call | solution.py:389
  3.7 0.5 collective-permute-start.3
  4.2 0.0 copy-start.5
  4.2 0.0 copy-start.8
  4.2 0.0 copy-start.9
  4.2 1.9 %shard_map.199.refs_0_ = bf16[144,128]{1,0:T(8,128)(2,1)S(1)} custom-call(s32[16]{0:T(128)} %bitcast.4, s32[16]{0:T(128)} %local.5, s32[16]{0:T(128)} %shift.5, f32[8,128,128]{2,1,0:T(8,128)} %theta.3, bf16[128,256]{1,0:T(8,128)(2,1)} %constant.41.clone.fy, bf16[96,128]{1,0:T(8,128)(2,1)} %constant.42.clone.fx), custom_call_target="tpu_custom_call" | custom-call | tf_op jit(solution)/shard_map/pallas_call | solution.py:389
  6.1 4.7 %collective-permute-start.2 = (bf16[144,128]{1,0:T(8,128)(2,1)S(1)}, bf16[144,128]{1,0:T(8,128)(2,1)S(1)}, u32[]{:S(2)}, u32[]{:S(2)}) collective-permute-start(bf16[144,128]{1,0:T(8,128)(2,1)S(1)} %shard_map.199.refs_0_), channel_id=1, source_target_pairs={{0,12},{4,0},{8,4},{12,8},{1,13},{5,1},{9,5},{13,9},{2,14},{6,2},{... | collective-permute-start | bytes 110600 | tf_op jit(solution)/shard_map/ppermute | solution.py:404
  10.8 1.0 %collective-permute-start = (bf16[144,128]{1,0:T(8,128)(2,1)S(1)}, bf16[144,128]{1,0:T(8,128)(2,1)S(1)}, u32[]{:S(2)}, u32[]{:S(2)}) collective-permute-start(bf16[144,128]{1,0:T(8,128)(2,1)S(1)} %shard_map.199.refs_0_), channel_id=1, source_target_pairs={{0,4},{4,8},{8,12},{12,0},{1,5},{5,9},{9,13},{13,1},{2,6},{6,10},{... | collective-permute-start | bytes 110600 | tf_op jit(solution)/shard_map/ppermute | solution.py:404
  11.8 0.7 %pad_add_fusion.at = s32[3]{0:T(128)} fusion(s32[1]{0:T(128)} %bitcast.2, s32[1]{0:T(128)} %bitcast.1, s32[1]{0:T(128)} %bitcast), kind=kLoop, calls=%fused_computation | loop fusion | flops 6 | bytes 24 | tf_op jit(solution)/shard_map/stack | solution.py:418
  12.5 0.2 collective-permute-done.2.refs_3_
  12.7 3.4 %collective-permute-done.1.refs_2_ = bf16[144,128]{1,0:T(8,128)(2,1)S(1)} collective-permute-done((bf16[144,128]{1,0:T(8,128)(2,1)S(1)}, bf16[144,128]{1,0:T(8,128)(2,1)S(1)}, u32[]{:S(2)}, u32[]{:S(2)}) %collective-permute-start.1) | collective-permute-done | bytes 36896 | tf_op jit(solution)/shard_map/ppermute | solution.py:404
  16.0 0.5 collective-permute-done.refs_1_
  16.6 0.0 copy-start.10
  16.6 0.0 copy-start.11
  16.6 0.0 copy-start.12
  16.7 2.8 %shard_map.201 = bf16[16,16,128]{2,1,0:T(8,128)(2,1)S(1)} custom-call(s32[3]{0:T(128)} %pad_add_fusion.at, s32[16]{0:T(128)} %bitcast.5, s32[16]{0:T(128)} %local.5, s32[16]{0:T(128)} %shift.5, bf16[144,128]{1,0:T(8,128)(2,1)S(1)} %shard_map.199.refs_0_, bf16[144,128]{1,0:T(8,128)(2,1)S(1)} %collective-permute-done.refs_1_, ...), custom_call_target="tpu_custom_call" | custom-call | tf_op jit(solution)/shard_map/pallas_call | solution.py:389
  19.5 0.0 copy-start.6
  19.5 0.0 copy-start.7
  19.5 10.4 %all_to_all.10.grads = bf16[16,16,128]{2,1,0:T(8,128)(2,1)S(1)} all-to-all(bf16[16,16,128]{2,1,0:T(8,128)(2,1)S(1)} %shard_map.201), channel_id=1, replica_groups=mesh['groups'=2,'cells'=4,'corners'=2,'kern'=2] {'cells','corners','kern'}, dimensions={0} | all-to-all | bytes 131072 | tf_op jit(solution)/shard_map/all_to_all | solution.py:455
  30.0 2.2 %shard_map.202 = (f32[8,128,128]{2,1,0:T(8,128)S(1)}, f32[8,8,256]{2,1,0:T(8,128)S(1)}, bf16[128,128]{1,0:T(8,128)(2,1)S(1)}) custom-call(s32[3]{0:T(128)} %pad_add_fusion.at, f32[8,128,128]{2,1,0:T(8,128)S(1)} %copy-done, bf16[16,16,128]{2,1,0:T(8,128)(2,1)S(1)} %all_to_all.10.grads, bf16[128,512]{1,0:T(8,128)(2,1)S(1)} %copy-done.10, ...), custom_call_target="tpu_custom_call" | custom-call | tf_op jit(solution)/shard_map/pallas_call | solution.py:389
  32.2 0.6 %collective-permute-start.6 = (bf16[128,128]{1,0:T(8,128)(2,1)S(1)}, bf16[128,128]{1,0:T(8,128)(2,1)S(1)}, u32[]{:S(2)}, u32[]{:S(2)}) collective-permute-start(bf16[128,128]{1,0:T(8,128)(2,1)S(1)} %get-tuple-element.9.refs_0_), channel_id=1, source_target_pairs={{0,12},{4,0},{8,4},{12,8},{1,13},{5,1},{9,5},{13,9},{2,14},{6,2},{... | collective-permute-start | bytes 98312 | tf_op jit(solution)/shard_map/ppermute | solution.py:404
  32.7 1.0 %collective-permute-start.5 = (bf16[128,128]{1,0:T(8,128)(2,1)S(1)}, bf16[128,128]{1,0:T(8,128)(2,1)S(1)}, u32[]{:S(2)}, u32[]{:S(2)}) collective-permute-start(bf16[128,128]{1,0:T(8,128)(2,1)S(1)} %get-tuple-element.9.refs_0_), channel_id=1, source_target_pairs={{0,8},{4,12},{8,0},{12,4},{1,9},{5,13},{9,1},{13,5},{2,10},{6,14},... | collective-permute-start | bytes 98312 | tf_op jit(solution)/shard_map/ppermute | solution.py:404
  33.8 0.7 %collective-permute-start.4 = (bf16[128,128]{1,0:T(8,128)(2,1)S(1)}, bf16[128,128]{1,0:T(8,128)(2,1)S(1)}, u32[]{:S(2)}, u32[]{:S(2)}) collective-permute-start(bf16[128,128]{1,0:T(8,128)(2,1)S(1)} %get-tuple-element.9.refs_0_), channel_id=1, source_target_pairs={{0,4},{4,8},{8,12},{12,0},{1,5},{5,9},{9,13},{13,1},{2,6},{6,10},{... | collective-permute-start | bytes 98312 | tf_op jit(solution)/shard_map/ppermute | solution.py:404
  34.4 1.7 %collective-permute-done.6.refs_3_ = bf16[128,128]{1,0:T(8,128)(2,1)S(1)} collective-permute-done((bf16[128,128]{1,0:T(8,128)(2,1)S(1)}, bf16[128,128]{1,0:T(8,128)(2,1)S(1)}, u32[]{:S(2)}, u32[]{:S(2)}) %collective-permute-start.6) | collective-permute-done | bytes 32800 | tf_op jit(solution)/shard_map/ppermute | solution.py:404
  36.1 1.4 %collective-permute-done.5.refs_2_ = bf16[128,128]{1,0:T(8,128)(2,1)S(1)} collective-permute-done((bf16[128,128]{1,0:T(8,128)(2,1)S(1)}, bf16[128,128]{1,0:T(8,128)(2,1)S(1)}, u32[]{:S(2)}, u32[]{:S(2)}) %collective-permute-start.5) | collective-permute-done | bytes 32800 | tf_op jit(solution)/shard_map/ppermute | solution.py:404
  37.5 1.9 %collective-permute-done.4.refs_1_ = bf16[128,128]{1,0:T(8,128)(2,1)S(1)} collective-permute-done((bf16[128,128]{1,0:T(8,128)(2,1)S(1)}, bf16[128,128]{1,0:T(8,128)(2,1)S(1)}, u32[]{:S(2)}, u32[]{:S(2)}) %collective-permute-start.4) | collective-permute-done | bytes 32800 | tf_op jit(solution)/shard_map/ppermute | solution.py:404
  39.5 2.7 %shard_map.203 = bf16[16,16,128]{2,1,0:T(8,128)(2,1)S(1)} custom-call(s32[3]{0:T(128)} %pad_add_fusion.at, s32[16]{0:T(128)} %bitcast.6, s32[16]{0:T(128)} %local.5, s32[16]{0:T(128)} %shift.5, bf16[128,128]{1,0:T(8,128)(2,1)S(1)} %get-tuple-element.9.refs_0_, bf16[128,128]{1,0:T(8,128)(2,1)S(1)} %collective-permute-done.4.refs_1_, ...), custom_call_target="tpu_custom_call" | custom-call | tf_op jit(solution)/shard_map/pallas_call | solution.py:389
  42.1 9.5 %all_to_all.11.grads = bf16[16,16,128]{2,1,0:T(8,128)(2,1)S(1)} all-to-all(bf16[16,16,128]{2,1,0:T(8,128)(2,1)S(1)} %shard_map.203), channel_id=1, replica_groups=mesh['groups'=2,'cells'=4,'corners'=2,'kern'=2] {'cells','corners','kern'}, dimensions={0} | all-to-all | bytes 131072 | tf_op jit(solution)/shard_map/all_to_all | solution.py:455
  51.6 2.0 %shard_map.204 = f32[8,32,128]{2,1,0:T(8,128)} custom-call(s32[3]{0:T(128)} %pad_add_fusion.at, f32[8,128,128]{2,1,0:T(8,128)S(1)} %get-tuple-element.8.theta, bf16[16,16,128]{2,1,0:T(8,128)(2,1)S(1)} %all_to_all.11.grads, f32[8,8,256]{2,1,0:T(8,128)S(1)} %get-tuple-element.10.sums, bf16[128,256]{1,0:T(8,128)(2,1)S(1)} %copy-done.6, ...), custom_call_target="tpu_custom_call" | custom-call | tf_op jit(solution)/shard_map/pallas_call | solution.py:389
  (24 shorter events, 0.0 us)
Async XLA Ops:
  0.7 1.1 %copy-start.14 = (bf16[4,35,128]{2,1,0:T(8,128)(2,1)S(1)}, bf16[4,35,128]{2,1,0:T(8,128)(2,1)}, u32[]{:S(2)}) copy-start(bf16[4,35,128]{2,1,0:T(8,128)(2,1)} %constant.44.clone.lane) | copy-start | bytes 107524
  0.7 1.1 %copy-start.15 = (bf16[2,24,35]{2,1,0:T(8,128)(2,1)S(1)}, bf16[2,24,35]{2,1,0:T(8,128)(2,1)}, u32[]{:S(2)}) copy-start(bf16[2,24,35]{2,1,0:T(8,128)(2,1)} %constant.43.clone.pick) | copy-start | bytes 10084
  3.7 12.8 %collective-permute-start.3 = (bf16[12,48,128]{2,1,0:T(8,128)(2,1)S(1)}, bf16[12,48,128]{2,1,0:T(8,128)(2,1)S(1)}, u32[]{:S(2)}, u32[]{:S(2)}) collective-permute-start(bf16[12,48,128]{2,1,0:T(8,128)(2,1)S(1)} %shard_map.200.refs_4_), channel_id=1, source_target_pairs={{0,1},{1,0},{2,3},{3,2},{4,5},{5,4},{6,7},{7,6},{8,9},{9,8},{10,11... | collective-permute-start | bytes 442376 | tf_op jit(solution)/shard_map/ppermute | solution.py:404
  4.2 12.3 %copy-start.1 = (bf16[256,256]{1,0:T(8,128)(2,1)S(1)}, bf16[256,256]{1,0:T(8,128)(2,1)}, u32[]{:S(2)}) copy-start(bf16[256,256]{1,0:T(8,128)(2,1)} %constant.47.clone.refs_9_) | copy-start | bytes 393220
  4.2 12.3 %copy-start.2 = (bf16[256,256]{1,0:T(8,128)(2,1)S(1)}, bf16[256,256]{1,0:T(8,128)(2,1)}, u32[]{:S(2)}) copy-start(bf16[256,256]{1,0:T(8,128)(2,1)} %constant.46.clone.refs_8_) | copy-start | bytes 393220
  4.2 12.4 %copy-start.3 = (f32[128,256]{1,0:T(8,128)S(1)}, f32[128,256]{1,0:T(8,128)}, u32[]{:S(2)}) copy-start(f32[128,256]{1,0:T(8,128)} %constant.45.clone.refs_7_) | copy-start | bytes 393220
  4.2 12.4 %copy-start.4 = (bf16[2,128,128]{2,1,0:T(8,128)(2,1)S(1)}, bf16[2,128,128]{2,1,0:T(8,128)(2,1)}, u32[]{:S(2)}) copy-start(bf16[2,128,128]{2,1,0:T(8,128)(2,1)} %refs_6_.3) | copy-start | bytes 196612
  4.2 12.4 %copy-start.5 = (bf16[128,224]{1,0:T(8,128)(2,1)S(1)}, bf16[128,224]{1,0:T(8,128)(2,1)}, u32[]{:S(2)}) copy-start(bf16[128,224]{1,0:T(8,128)(2,1)} %constant.50.clone.refs_12_) | copy-start | bytes 172036
  4.2 12.4 %copy-start.8 = (bf16[96,144]{1,0:T(8,128)(2,1)S(1)}, bf16[96,144]{1,0:T(8,128)(2,1)}, u32[]{:S(2)}) copy-start(bf16[96,144]{1,0:T(8,128)(2,1)} %constant.49.clone.refs_11_) | copy-start | bytes 82948
  4.2 12.4 %copy-start.9 = (bf16[144,96]{1,0:T(8,128)(2,1)S(1)}, bf16[144,96]{1,0:T(8,128)(2,1)}, u32[]{:S(2)}) copy-start(bf16[144,96]{1,0:T(8,128)(2,1)} %constant.48.clone.refs_10_) | copy-start | bytes 82948
  6.1 10.5 %copy-start.13 = (bf16[72,128]{1,0:T(8,128)(2,1)S(1)}, bf16[72,128]{1,0:T(8,128)(2,1)}, u32[]{:S(2)}) copy-start(bf16[72,128]{1,0:T(8,128)(2,1)} %constant.51.clone.refs_13_) | copy-start | bytes 55300
  6.1 6.5 %collective-permute-start.2 = (bf16[144,128]{1,0:T(8,128)(2,1)S(1)}, bf16[144,128]{1,0:T(8,128)(2,1)S(1)}, u32[]{:S(2)}, u32[]{:S(2)}) collective-permute-start(bf16[144,128]{1,0:T(8,128)(2,1)S(1)} %shard_map.199.refs_0_), channel_id=1, source_target_pairs={{0,12},{4,0},{8,4},{12,8},{1,13},{5,1},{9,5},{13,9},{2,14},{6,2},{... | collective-permute-start | bytes 110600 | tf_op jit(solution)/shard_map/ppermute | solution.py:404
  10.8 5.3 %collective-permute-start.1 = (bf16[144,128]{1,0:T(8,128)(2,1)S(1)}, bf16[144,128]{1,0:T(8,128)(2,1)S(1)}, u32[]{:S(2)}, u32[]{:S(2)}) collective-permute-start(bf16[144,128]{1,0:T(8,128)(2,1)S(1)} %shard_map.199.refs_0_), channel_id=1, source_target_pairs={{0,8},{4,12},{8,0},{12,4},{1,9},{5,13},{9,1},{13,5},{2,10},{6,14},... | collective-permute-start | bytes 110600 | tf_op jit(solution)/shard_map/ppermute | solution.py:404
  10.8 5.8 %collective-permute-start = (bf16[144,128]{1,0:T(8,128)(2,1)S(1)}, bf16[144,128]{1,0:T(8,128)(2,1)S(1)}, u32[]{:S(2)}, u32[]{:S(2)}) collective-permute-start(bf16[144,128]{1,0:T(8,128)(2,1)S(1)} %shard_map.199.refs_0_), channel_id=1, source_target_pairs={{0,4},{4,8},{8,12},{12,0},{1,5},{5,9},{9,13},{13,1},{2,6},{6,10},{... | collective-permute-start | bytes 110600 | tf_op jit(solution)/shard_map/ppermute | solution.py:404
  12.5 17.5 %copy-start = (f32[8,128,128]{2,1,0:T(8,128)S(1)}, f32[8,128,128]{2,1,0:T(8,128)}, u32[]{:S(2)}) copy-start(f32[8,128,128]{2,1,0:T(8,128)} %theta.3) | copy-start | bytes 1572868
  16.6 13.3 %copy-start.10 = (bf16[128,512]{1,0:T(8,128)(2,1)S(1)}, bf16[128,512]{1,0:T(8,128)(2,1)}, u32[]{:S(2)}) copy-start(bf16[128,512]{1,0:T(8,128)(2,1)} %constant.52.clone.ph) | copy-start | bytes 393220
  16.6 13.3 %copy-start.11 = (bf16[128,48]{1,0:T(8,128)(2,1)S(1)}, bf16[128,48]{1,0:T(8,128)(2,1)}, u32[]{:S(2)}) copy-start(bf16[128,48]{1,0:T(8,128)(2,1)} %constant.54.clone.ex) | copy-start | bytes 36868
  16.6 13.3 %copy-start.12 = (bf16[96,128]{1,0:T(8,128)(2,1)S(1)}, bf16[96,128]{1,0:T(8,128)(2,1)}, u32[]{:S(2)}) copy-start(bf16[96,128]{1,0:T(8,128)(2,1)} %constant.42.clone.fx) | copy-start | bytes 73732
  19.5 10.5 %copy-start.6 = (bf16[128,256]{1,0:T(8,128)(2,1)S(1)}, bf16[128,256]{1,0:T(8,128)(2,1)}, u32[]{:S(2)}) copy-start(bf16[128,256]{1,0:T(8,128)(2,1)} %constant.53.clone.gy) | copy-start | bytes 196612
  19.5 10.5 %copy-start.7 = (bf16[128,256]{1,0:T(8,128)(2,1)S(1)}, bf16[128,256]{1,0:T(8,128)(2,1)}, u32[]{:S(2)}) copy-start(bf16[128,256]{1,0:T(8,128)(2,1)} %constant.41.clone.fy) | copy-start | bytes 196612
  32.2 3.9 %collective-permute-start.6 = (bf16[128,128]{1,0:T(8,128)(2,1)S(1)}, bf16[128,128]{1,0:T(8,128)(2,1)S(1)}, u32[]{:S(2)}, u32[]{:S(2)}) collective-permute-start(bf16[128,128]{1,0:T(8,128)(2,1)S(1)} %get-tuple-element.9.refs_0_), channel_id=1, source_target_pairs={{0,12},{4,0},{8,4},{12,8},{1,13},{5,1},{9,5},{13,9},{2,14},{6,2},{... | collective-permute-start | bytes 98312 | tf_op jit(solution)/shard_map/ppermute | solution.py:404
  32.7 4.8 %collective-permute-start.5 = (bf16[128,128]{1,0:T(8,128)(2,1)S(1)}, bf16[128,128]{1,0:T(8,128)(2,1)S(1)}, u32[]{:S(2)}, u32[]{:S(2)}) collective-permute-start(bf16[128,128]{1,0:T(8,128)(2,1)S(1)} %get-tuple-element.9.refs_0_), channel_id=1, source_target_pairs={{0,8},{4,12},{8,0},{12,4},{1,9},{5,13},{9,1},{13,5},{2,10},{6,14},... | collective-permute-start | bytes 98312 | tf_op jit(solution)/shard_map/ppermute | solution.py:404
  33.8 5.7 %collective-permute-start.4 = (bf16[128,128]{1,0:T(8,128)(2,1)S(1)}, bf16[128,128]{1,0:T(8,128)(2,1)S(1)}, u32[]{:S(2)}, u32[]{:S(2)}) collective-permute-start(bf16[128,128]{1,0:T(8,128)(2,1)S(1)} %get-tuple-element.9.refs_0_), channel_id=1, source_target_pairs={{0,4},{4,8},{8,12},{12,0},{1,5},{5,9},{9,13},{13,1},{2,6},{6,10},{... | collective-permute-start | bytes 98312 | tf_op jit(solution)/shard_map/ppermute | solution.py:404

commit v2 on v1

--- a/solution.py
+++ b/solution.py
@@ -89,19 +89,6 @@
         ph[:, LANES + HALF : LANES + HALF + freq] = -np.sin(phase)
         self.ph = ph.astype(np.float32)
         self.ph_split = np.concatenate(split(ph), axis=1)
-        pick_u, pick_v = np.zeros((rows, freq)), np.zeros((rows, freq))
-        for row in range(mid + 1):
-            pick_u[row, mid + row] = 1.0
-            if row > 0:
-                pick_v[row, mid - row] = 1.0
-        self.pick = np.stack([pick_u, pick_v]).astype(np.float32).astype(BF)
-        lane = np.zeros((4, freq, LANES))
-        for col in range(freq):
-            lane[0, col, col] = 1.0
-            lane[1, col, HALF + col] = 1.0
-            lane[2, col, freq - 1 - col] = 1.0
-            lane[3, col, HALF + freq - 1 - col] = -1.0
-        self.lane = lane.astype(np.float32).astype(BF)
 
 
 def packing(tabs):
@@ -167,15 +154,38 @@
     return lax.broadcasted_iota(jnp.int32, shape, len(shape) - 1)
 
 
-def arrange_body(dose, kern, pick, lane, out):
+def arrange_body(tabs, dose, kern, out):
+    freq, mid, rows = tabs.freq, tabs.mid, tabs.rows
+    number, tall = out.shape[0], up(freq, 8)
     root = jnp.sqrt(jnp.full((1, 1), dose[0], F32))
-    for k in range(out.shape[0]):
-        real = (kern[0, 0, k] * root).astype(BF)
-        imag = (kern[1, 0, k] * root).astype(BF)
-        upper = (dot(real, lane[0]) + dot(imag, lane[1])).astype(BF)
-        lower = (dot(real, lane[2]) + dot(imag, lane[3])).astype(BF)
-        both = jnp.concatenate([dot(pick[0], upper), dot(pick[1], lower)], axis=0)
-        out[k] = both.astype(BF)
+    side = jnp.zeros((freq, HALF - freq), F32)
+    below = jnp.zeros((tall - freq, LANES), F32)
+    rights = []
+    for k in range(number):
+        both = jnp.concatenate([kern[0, 0, k] * root, side, kern[1, 0, k] * root, side], axis=1)
+        rights.append(jnp.concatenate([both, below], axis=0))
+    rights = jnp.concatenate(rights, axis=0).astype(BF)
+    row = lax.broadcasted_iota(jnp.int32, (LANES, LANES), 0)
+    col = lane_of((LANES, LANES))
+    same = (row // HALF == col // HALF) & (row % HALF + col % HALF == freq - 1)
+    turned = jnp.where(same, jnp.where(row < HALF, 1.0, -1.0), 0.0).astype(BF)
+    lefts = dot(rights, turned)
+    rights = rights.astype(F32)
+    row = lax.broadcasted_iota(jnp.int32, (2 * rows, 2 * tall), 0)
+    col = lane_of((2 * rows, 2 * tall))
+    upper = (row <= mid) & (col == mid + row)
+    lower = (row > rows) & (row <= rows + mid) & (col == tall + mid - (row - rows))
+    pick = jnp.where(upper | lower, 1.0, 0.0).astype(BF)
+    for k in range(0, number, 2):
+        columns = [
+            jnp.concatenate(
+                [rights[m * tall : (m + 1) * tall], lefts[m * tall : (m + 1) * tall]], axis=0
+            )
+            for m in range(k, min(k + 2, number))
+        ]
+        res = dot(pick, jnp.concatenate(columns, axis=1).astype(BF)).astype(BF)
+        for p in range(len(columns)):
+            out[k + p] = res[:, p * LANES : (p + 1) * LANES]
 
 
 def spectra(tabs, slots, theta, fy, fx, out):
@@ -210,8 +220,8 @@
     out[base : base + INFO] = info.astype(F32).astype(BF)
 
 
-def counts(tabs, n, tiles, cells, slots, at, ph, payload, out):
-    z = at[0]
+def counts(tabs, n, tiles, cells, slots, ph, payload, out):
+    z = lax.axis_index("cells")
     base = cells * packing(tabs)[0]
     row = lax.broadcasted_iota(jnp.int32, (tiles * cells, LANES), 0)
     col = lane_of((tiles * cells, LANES))
@@ -230,25 +240,25 @@
     sums = dot(jnp.concatenate(numbers, axis=0).astype(BF), ph[...])
     sums = sums[:, : 2 * LANES] + sums[:, 2 * LANES :]
     for k in range(n):
-        source = lax.rem(z - k + n, n)
+        place = source(n, z, k)
         part = sums[k * tiles * cells : (k + 1) * tiles * cells]
-        out[pl.ds(source * tiles, tiles)] = part.reshape(tiles, cells, 2 * LANES)
-
-
-def tile_body(tabs, n, cells, tiles, copies, at, owner, local, shift, *refs):
+        out[pl.ds(place * tiles, tiles)] = part.reshape(tiles, cells, 2 * LANES)
+
+
+def tile_body(tabs, n, cells, tiles, copies, owner, local, shift, *refs):
     payload, refs = refs[:n], refs[n:]
     arranged, refs = refs[:tiles], refs[tiles:]
     target, ph, gyy, gyy_t, gx, gx_t, w, w_t, out, held, wide, tall, near = refs
     rows, cell, grid = tabs.rows, tabs.cell, tabs.grid
     slots = local.shape[0] // tiles
-    z, j = at[0], at[1]
+    z, j = lax.axis_index("cells"), lax.axis_index("kern")
     for k in range(n):
         sent = packing(tabs)[0]
         held[pl.ds(k * cells, cells)] = payload[k][0 : cells * sent].reshape(cells, sent, LANES)
     spec = jnp.zeros((rows, LANES), F32)
     for s in range(slots):
         i = j * slots + s
-        which = lax.rem(z - owner[i] + n, n) * cells + local[i]
+        which = source(n, z, owner[i]) * cells + local[i]
         one = unpack(tabs, held[which])
         turn = ph[pl.ds(shift[i], 1)]
         spec = spec + one * turn[:, :LANES] + swap(one) * turn[:, LANES:]
@@ -350,9 +360,9 @@
     return result
 
 
-def update_body(tabs, slots, corners, kern, n, at, theta, grads, ph, gy, ex, fy, fx, *refs):
+def update_body(tabs, slots, corners, kern, n, theta, grads, ph, gy, ex, fy, fx, *refs):
     heard, (out, sums, payload) = refs[:n], refs[n:]
-    counts(tabs, n, kern, theta.shape[0], slots, at, ph, heard, sums)
+    counts(tabs, n, kern, theta.shape[0], slots, ph, heard, sums)
     for c, (gradient, rate) in enumerate(
         gradients(tabs, slots, corners, kern, theta, grads, sums, gy, ex)
     ):
@@ -360,9 +370,9 @@
     spectra(tabs, slots, out[...], fy, fx, payload)
 
 
-def last_body(tabs, slots, corners, kern, at, theta, grads, sums, gy, ex, out, held, ready, sem):
+def last_body(tabs, slots, corners, kern, theta, grads, sums, gy, ex, out, held, ready, sem):
     band = out.shape[1]
-    start = pl.multiple_of(at[2] * band, band)
+    start = pl.multiple_of(lax.axis_index(("corners", "kern")) * band, band)
     copies = []
     for c, (gradient, rate) in enumerate(
         gradients(tabs, slots, corners, kern, theta, grads, sums, gy, ex)
@@ -399,9 +409,18 @@
     return pltpu.VMEM(dims, dtype)
 
 
+def paired(n):
+    return n & (n - 1) == 0
+
+
+def source(n, z, step):
+    return z ^ step if paired(n) else lax.rem(z - step + n, n)
+
+
 def shifted(array, axis, step):
     n = lax.axis_size(axis)
-    return lax.ppermute(array, axis, [(i, (i + step) % n) for i in range(n)])
+    moves = [(i, i ^ step if paired(n) else (i + step) % n) for i in range(n)]
+    return lax.ppermute(array, axis, moves)
 
 
 def per_device(theta, target, kernels, dose, inst_owner, inst_local, inst_shift):
@@ -415,9 +434,6 @@
     tabs = Tables(cell, kernels.shape[3])
     inst_owner = inst_owner[:, 0]
     rows, sent = tabs.rows, packing(tabs)[0]
-    at = jnp.stack(
-        [lax.axis_index("cells"), lax.axis_index("kern"), lax.axis_index(("corners", "kern"))]
-    ).astype(jnp.int32)
     band = cell // (n_kern * n_corners)
     payload = call(
         functools.partial(first_body, tabs, slots),
@@ -430,9 +446,9 @@
     for k in range(1, n):
         payloads.append(shifted(payload, "cells", k))
     own = call(
-        arrange_body,
+        functools.partial(arrange_body, tabs),
         [dose],
-        [kernels, tabs.pick, tabs.lane],
+        [kernels],
         shape((kernels.shape[2], 2 * rows, LANES), BF),
     )
     arranged = [own] + [shifted(own, "kern", k) for k in range(1, n_kern)]
@@ -440,7 +456,7 @@
     for iteration in range(ITERS):
         grads = call(
             functools.partial(tile_body, tabs, n, cells, tiles, copies),
-            [at, inst_owner, inst_local, inst_shift],
+            [inst_owner, inst_local, inst_shift],
             payloads
             + arranged
             + [target, tabs.ph, tabs.gyy, tabs.gyy_t, tabs.gx, tabs.gx_t, tabs.w, tabs.w_t],
@@ -456,7 +472,7 @@
         if iteration == ITERS - 1:
             return call(
                 functools.partial(last_body, tabs, slots, n_corners, n_kern),
-                [at],
+                [],
                 [theta, grads, sums, tabs.gy, tabs.ex],
                 jax.ShapeDtypeStruct((cells, band, cell), F32),
                 scratch=[
@@ -468,7 +484,7 @@
             )
         theta, sums, payload = call(
             functools.partial(update_body, tabs, slots, n_corners, n_kern, n),
-            [at],
+            [],
             [theta, grads, tabs.ph_split, tabs.gy, tabs.ex, tabs.fy, tabs.fx] + payloads,
             [
                 shape(theta.shape, F32),
@@ -476,7 +492,9 @@
                 shape((cells * sent, LANES), BF),
             ],
         )
-        payloads = [payload] + [shifted(payload, "cells", k) for k in range(1, n)]
+        payloads = [payload]
+        for k in range(1, n):
+            payloads.append(shifted(payload, "cells", k))
 
 
 def solution(mesh):

time: 53.9 us -> 50.9 us (0.944)
  waiting for transfers between devices: 9.14 us -> 6.11 us
  Pallas kernels: 13.5 us -> 10.6 us
  starting transfers between devices: 8.44 us -> 10.4 us
  blocking collectives: 19.9 us -> 21.6 us
  other arithmetic: 0.67 us -> 0 us
    ppermute x7, waiting for transfers between devices: 9.14 us -> 6.11 us  [shifted(): return lax.ppermute(array, axis, moves)]
    pallas_call x6, Pallas kernels: 13.5 us -> 10.6 us  [call(): pl.pallas_call(body, out_shape=outs, in_specs=[SMEM] * len(scalars) + [VM...]
    ppermute x7, starting transfers between devices: 8.44 us -> 10.4 us  [shifted(): return lax.ppermute(array, axis, moves)]
    all_to_all x2, blocking collectives: 19.9 us -> 21.6 us  [per_device(): lax.all_to_all(grads, ('cells', 'corners', 'kern'), 0, 0, tiled=True)]
    another operation x1 -> x0, other arithmetic: 0.67 us -> none  [per_device(): jnp.stack([lax.axis_index('cells'), lax.axis_index('kern'), lax.axis_inde...]
    unnamed x33 -> x29, local copies, waits for them, and re-layouts: 1.14 us -> 1.13 us
  transfers between devices with their start and end apart: 7 -> 7, of which waited for: 6 -> 4; matrix products, arithmetic and copies ran while one was open for 1% -> 0% of each run, Pallas kernels for 3% -> 4%
where the time goes in v2:
time: 50.9 us; the launch traced here: 50.6 us
  blocking collectives  21.6 us (42%)
  Pallas kernels  10.6 us (21%)
  starting transfers between devices  10.4 us (20%)
  waiting for transfers between devices  6.11 us (12%)
  local copies, waits for them, and re-layouts  1.13 us (2%)
  between operations  0.85 us (2%)
    all_to_all x2, blocking collectives, per_device(): lax.all_to_all(grads, ('cells', 'corners', 'kern'), 0, 0, tiled=True)  21.6 us
    pallas_call x6, Pallas kernels, call(): pl.pallas_call(body, out_shape=outs, in_specs=[SMEM] * len(scalars) + [VM...  10.6 us
    ppermute x7, starting transfers between devices, shifted(): return lax.ppermute(array, axis, moves)  10.4 us
    ppermute x7, waiting for transfers between devices, shifted(): return lax.ppermute(array, axis, moves)  6.11 us
    unnamed x29, local copies, waits for them, and re-layouts  1.13 us
  transfers between devices with their start and end apart: 7, of which 4 were waited for; matrix products, arithmetic and copies ran while one was open for 0% of the time, Pallas kernels for 4%

profile of v2, /device:TPU:0, one launch (start us, length us, event | category | flops | bytes accessed | tf_op | source)
XLA Modules:
  0.0 50.6 jit_solution(6915424531205703120)
XLA Ops:
  0.7 1.0 %copy.20.kern = f32[2,1,12,35,35]{4,3,2,1,0:T(8,128)S(1)} copy(f32[2,1,12,35,35]{4,1,3,2,0:T(1,128)} %param.21) | data formatting | bytes 235200 | tf_op args[2]
  1.7 0.4 shard_map.182.refs_4_
  2.1 0.6 %collective-permute-start.3 = (bf16[12,48,128]{2,1,0:T(8,128)(2,1)S(1)}, bf16[12,48,128]{2,1,0:T(8,128)(2,1)S(1)}, u32[]{:S(2)}, u32[]{:S(2)}) collective-permute-start(bf16[12,48,128]{2,1,0:T(8,128)(2,1)S(1)} %shard_map.182.refs_4_), channel_id=1, source_target_pairs={{0,1},{1,0},{2,3},{3,2},{4,5},{5,4},{6,7},{7,6},{8,9},{9,8},{10,11... | collective-permute-start | bytes 442376 | tf_op jit(solution)/shard_map/ppermute | solution.py:423
  2.7 0.0 copy-start.6
  2.7 0.0 copy-start.8
  2.7 0.0 copy-start.9
  2.7 0.0 copy-start.13
  2.7 1.9 %shard_map.181.refs_0_ = bf16[144,128]{1,0:T(8,128)(2,1)S(1)} custom-call(s32[16]{0:T(128)} %bitcast.1, s32[16]{0:T(128)} %local.5, s32[16]{0:T(128)} %shift.5, f32[8,128,128]{2,1,0:T(8,128)} %theta.3, bf16[128,256]{1,0:T(8,128)(2,1)} %constant.24.clone.fy, bf16[96,128]{1,0:T(8,128)(2,1)} %constant.25.clone.fx), custom_call_target="tpu_custom_call" | custom-call | tf_op jit(solution)/shard_map/pallas_call | solution.py:399
  4.6 4.7 %collective-permute-start.2 = (bf16[144,128]{1,0:T(8,128)(2,1)S(1)}, bf16[144,128]{1,0:T(8,128)(2,1)S(1)}, u32[]{:S(2)}, u32[]{:S(2)}) collective-permute-start(bf16[144,128]{1,0:T(8,128)(2,1)S(1)} %shard_map.181.refs_0_), channel_id=1, source_target_pairs={{0,12},{4,8},{8,4},{12,0},{1,13},{5,9},{9,5},{13,1},{2,14},{6,10},... | collective-permute-start | bytes 110600 | tf_op jit(solution)/shard_map/ppermute | solution.py:423
  9.3 0.0 collective-permute-start.1
  9.3 0.6 %collective-permute-start = (bf16[144,128]{1,0:T(8,128)(2,1)S(1)}, bf16[144,128]{1,0:T(8,128)(2,1)S(1)}, u32[]{:S(2)}, u32[]{:S(2)}) collective-permute-start(bf16[144,128]{1,0:T(8,128)(2,1)S(1)} %shard_map.181.refs_0_), channel_id=1, source_target_pairs={{0,4},{4,0},{8,12},{12,8},{1,5},{5,1},{9,13},{13,9},{2,6},{6,2},{1... | collective-permute-start | bytes 110600 | tf_op jit(solution)/shard_map/ppermute | solution.py:423
  10.0 1.5 %collective-permute-done.2.refs_3_ = bf16[144,128]{1,0:T(8,128)(2,1)S(1)} collective-permute-done((bf16[144,128]{1,0:T(8,128)(2,1)S(1)}, bf16[144,128]{1,0:T(8,128)(2,1)S(1)}, u32[]{:S(2)}, u32[]{:S(2)}) %collective-permute-start.2) | collective-permute-done | bytes 36896 | tf_op jit(solution)/shard_map/ppermute | solution.py:423
  11.5 2.7 %collective-permute-done.1.refs_2_ = bf16[144,128]{1,0:T(8,128)(2,1)S(1)} collective-permute-done((bf16[144,128]{1,0:T(8,128)(2,1)S(1)}, bf16[144,128]{1,0:T(8,128)(2,1)S(1)}, u32[]{:S(2)}, u32[]{:S(2)}) %collective-permute-start.1) | collective-permute-done | bytes 36896 | tf_op jit(solution)/shard_map/ppermute | solution.py:423
  14.2 0.0 collective-permute-done.refs_1_
  14.2 0.0 collective-permute-done.3.refs_5_
  14.3 0.0 copy-start.10
  14.3 0.0 copy-start.11
  14.3 0.0 copy-start.12
  14.3 2.8 %shard_map.183 = bf16[16,16,128]{2,1,0:T(8,128)(2,1)S(1)} custom-call(s32[16]{0:T(128)} %bitcast.2, s32[16]{0:T(128)} %local.5, s32[16]{0:T(128)} %shift.5, bf16[144,128]{1,0:T(8,128)(2,1)S(1)} %shard_map.181.refs_0_, bf16[144,128]{1,0:T(8,128)(2,1)S(1)} %collective-permute-done.refs_1_, bf16[144,128]{1,0:T(8,128)(2,1)S(1)} %collective-permute-done.1.refs_2_, ...), custom_call_target="tpu_custom_call" | custom-call | tf_op jit(solution)/shard_map/pallas_call | solution.py:399
  17.1 0.0 copy-start.5
  17.1 0.0 copy-start.7
  17.1 11.2 %all_to_all.10.grads = bf16[16,16,128]{2,1,0:T(8,128)(2,1)S(1)} all-to-all(bf16[16,16,128]{2,1,0:T(8,128)(2,1)S(1)} %shard_map.183), channel_id=1, replica_groups=mesh['groups'=2,'cells'=4,'corners'=2,'kern'=2] {'cells','corners','kern'}, dimensions={0} | all-to-all | bytes 131072 | tf_op jit(solution)/shard_map/all_to_all | solution.py:471
  28.3 1.5 %shard_map.184 = (f32[8,128,128]{2,1,0:T(8,128)S(1)}, f32[8,8,256]{2,1,0:T(8,128)S(1)}, bf16[128,128]{1,0:T(8,128)(2,1)S(1)}) custom-call(f32[8,128,128]{2,1,0:T(8,128)S(1)} %copy-done, bf16[16,16,128]{2,1,0:T(8,128)(2,1)S(1)} %all_to_all.10.grads, bf16[128,512]{1,0:T(8,128)(2,1)S(1)} %copy-done.11, bf16[128,256]{1,0:T(8,128)(2,1)S(1)} %copy-done.5, ...), custom_call_target="tpu_custom_call" | custom-call | tf_op jit(solution)/shard_map/pallas_call | solution.py:399
  29.8 0.6 %collective-permute-start.6 = (bf16[128,128]{1,0:T(8,128)(2,1)S(1)}, bf16[128,128]{1,0:T(8,128)(2,1)S(1)}, u32[]{:S(2)}, u32[]{:S(2)}) collective-permute-start(bf16[128,128]{1,0:T(8,128)(2,1)S(1)} %get-tuple-element.9.refs_0_), channel_id=1, source_target_pairs={{0,12},{4,8},{8,4},{12,0},{1,13},{5,9},{9,5},{13,1},{2,14},{6,10},... | collective-permute-start | bytes 98312 | tf_op jit(solution)/shard_map/ppermute | solution.py:423
  30.4 1.0 %collective-permute-start.5 = (bf16[128,128]{1,0:T(8,128)(2,1)S(1)}, bf16[128,128]{1,0:T(8,128)(2,1)S(1)}, u32[]{:S(2)}, u32[]{:S(2)}) collective-permute-start(bf16[128,128]{1,0:T(8,128)(2,1)S(1)} %get-tuple-element.9.refs_0_), channel_id=1, source_target_pairs={{0,8},{4,12},{8,0},{12,4},{1,9},{5,13},{9,1},{13,5},{2,10},{6,14},... | collective-permute-start | bytes 98312 | tf_op jit(solution)/shard_map/ppermute | solution.py:423
  31.5 2.8 %collective-permute-start.4 = (bf16[128,128]{1,0:T(8,128)(2,1)S(1)}, bf16[128,128]{1,0:T(8,128)(2,1)S(1)}, u32[]{:S(2)}, u32[]{:S(2)}) collective-permute-start(bf16[128,128]{1,0:T(8,128)(2,1)S(1)} %get-tuple-element.9.refs_0_), channel_id=1, source_target_pairs={{0,4},{4,0},{8,12},{12,8},{1,5},{5,1},{9,13},{13,9},{2,6},{6,2},{1... | collective-permute-start | bytes 98312 | tf_op jit(solution)/shard_map/ppermute | solution.py:423
  34.3 1.4 %collective-permute-done.6.refs_3_ = bf16[128,128]{1,0:T(8,128)(2,1)S(1)} collective-permute-done((bf16[128,128]{1,0:T(8,128)(2,1)S(1)}, bf16[128,128]{1,0:T(8,128)(2,1)S(1)}, u32[]{:S(2)}, u32[]{:S(2)}) %collective-permute-start.6) | collective-permute-done | bytes 32800 | tf_op jit(solution)/shard_map/ppermute | solution.py:423
  35.6 0.0 collective-permute-done.5.refs_2_
  35.6 0.5 %collective-permute-done.4.refs_1_ = bf16[128,128]{1,0:T(8,128)(2,1)S(1)} collective-permute-done((bf16[128,128]{1,0:T(8,128)(2,1)S(1)}, bf16[128,128]{1,0:T(8,128)(2,1)S(1)}, u32[]{:S(2)}, u32[]{:S(2)}) %collective-permute-start.4) | collective-permute-done | bytes 32800 | tf_op jit(solution)/shard_map/ppermute | solution.py:423
  36.2 2.6 %shard_map.185 = bf16[16,16,128]{2,1,0:T(8,128)(2,1)S(1)} custom-call(s32[16]{0:T(128)} %bitcast.3, s32[16]{0:T(128)} %local.5, s32[16]{0:T(128)} %shift.5, bf16[128,128]{1,0:T(8,128)(2,1)S(1)} %get-tuple-element.9.refs_0_, bf16[128,128]{1,0:T(8,128)(2,1)S(1)} %collective-permute-done.4.refs_1_, bf16[128,128]{1,0:T(8,128)(2,1)S(1)} %collective-permute-done.5.refs_2_, ...), custom_call_target="tpu_custom_call" | custom-call | tf_op jit(solution)/shard_map/pallas_call | solution.py:399
  38.8 10.4 %all_to_all.11.grads = bf16[16,16,128]{2,1,0:T(8,128)(2,1)S(1)} all-to-all(bf16[16,16,128]{2,1,0:T(8,128)(2,1)S(1)} %shard_map.185), channel_id=1, replica_groups=mesh['groups'=2,'cells'=4,'corners'=2,'kern'=2] {'cells','corners','kern'}, dimensions={0} | all-to-all | bytes 131072 | tf_op jit(solution)/shard_map/all_to_all | solution.py:471
  49.2 1.3 %shard_map.186 = f32[8,32,128]{2,1,0:T(8,128)} custom-call(f32[8,128,128]{2,1,0:T(8,128)S(1)} %get-tuple-element.8.theta, bf16[16,16,128]{2,1,0:T(8,128)(2,1)S(1)} %all_to_all.11.grads, f32[8,8,256]{2,1,0:T(8,128)S(1)} %get-tuple-element.10.sums, bf16[128,256]{1,0:T(8,128)(2,1)S(1)} %copy-done.5, bf16[128,48]{1,0:T(8,128)(2,1)S(1)} %copy-done.10), custom_call_target="tpu_custom_call" | custom-call | tf_op jit(solution)/shard_map/pallas_call | solution.py:399
  (19 shorter events, 0.0 us)
Async XLA Ops:
  2.1 12.1 %collective-permute-start.3 = (bf16[12,48,128]{2,1,0:T(8,128)(2,1)S(1)}, bf16[12,48,128]{2,1,0:T(8,128)(2,1)S(1)}, u32[]{:S(2)}, u32[]{:S(2)}) collective-permute-start(bf16[12,48,128]{2,1,0:T(8,128)(2,1)S(1)} %shard_map.182.refs_4_), channel_id=1, source_target_pairs={{0,1},{1,0},{2,3},{3,2},{4,5},{5,4},{6,7},{7,6},{8,9},{9,8},{10,11... | collective-permute-start | bytes 442376 | tf_op jit(solution)/shard_map/ppermute | solution.py:423
  2.7 11.5 %copy-start.1 = (bf16[256,256]{1,0:T(8,128)(2,1)S(1)}, bf16[256,256]{1,0:T(8,128)(2,1)}, u32[]{:S(2)}) copy-start(bf16[256,256]{1,0:T(8,128)(2,1)} %constant.28.clone.refs_9_) | copy-start | bytes 393220
  2.7 11.5 %copy-start.2 = (bf16[256,256]{1,0:T(8,128)(2,1)S(1)}, bf16[256,256]{1,0:T(8,128)(2,1)}, u32[]{:S(2)}) copy-start(bf16[256,256]{1,0:T(8,128)(2,1)} %constant.27.clone.refs_8_) | copy-start | bytes 393220
  2.7 11.6 %copy-start.3 = (f32[128,256]{1,0:T(8,128)S(1)}, f32[128,256]{1,0:T(8,128)}, u32[]{:S(2)}) copy-start(f32[128,256]{1,0:T(8,128)} %constant.26.clone.refs_7_) | copy-start | bytes 393220
  2.7 11.6 %copy-start.4 = (bf16[2,128,128]{2,1,0:T(8,128)(2,1)S(1)}, bf16[2,128,128]{2,1,0:T(8,128)(2,1)}, u32[]{:S(2)}) copy-start(bf16[2,128,128]{2,1,0:T(8,128)(2,1)} %refs_6_.3) | copy-start | bytes 196612
  2.7 11.6 %copy-start.6 = (bf16[128,224]{1,0:T(8,128)(2,1)S(1)}, bf16[128,224]{1,0:T(8,128)(2,1)}, u32[]{:S(2)}) copy-start(bf16[128,224]{1,0:T(8,128)(2,1)} %constant.31.clone.refs_12_) | copy-start | bytes 172036
  2.7 11.6 %copy-start.8 = (bf16[96,144]{1,0:T(8,128)(2,1)S(1)}, bf16[96,144]{1,0:T(8,128)(2,1)}, u32[]{:S(2)}) copy-start(bf16[96,144]{1,0:T(8,128)(2,1)} %constant.30.clone.refs_11_) | copy-start | bytes 82948
  2.7 11.6 %copy-start.9 = (bf16[144,96]{1,0:T(8,128)(2,1)S(1)}, bf16[144,96]{1,0:T(8,128)(2,1)}, u32[]{:S(2)}) copy-start(bf16[144,96]{1,0:T(8,128)(2,1)} %constant.29.clone.refs_10_) | copy-start | bytes 82948
  2.7 11.6 %copy-start.13 = (bf16[72,128]{1,0:T(8,128)(2,1)S(1)}, bf16[72,128]{1,0:T(8,128)(2,1)}, u32[]{:S(2)}) copy-start(bf16[72,128]{1,0:T(8,128)(2,1)} %constant.32.clone.refs_13_) | copy-start | bytes 55300
  4.6 23.7 %copy-start = (f32[8,128,128]{2,1,0:T(8,128)S(1)}, f32[8,128,128]{2,1,0:T(8,128)}, u32[]{:S(2)}) copy-start(f32[8,128,128]{2,1,0:T(8,128)} %theta.3) | copy-start | bytes 1572868
  4.6 6.9 %collective-permute-start.2 = (bf16[144,128]{1,0:T(8,128)(2,1)S(1)}, bf16[144,128]{1,0:T(8,128)(2,1)S(1)}, u32[]{:S(2)}, u32[]{:S(2)}) collective-permute-start(bf16[144,128]{1,0:T(8,128)(2,1)S(1)} %shard_map.181.refs_0_), channel_id=1, source_target_pairs={{0,12},{4,8},{8,4},{12,0},{1,13},{5,9},{9,5},{13,1},{2,14},{6,10},... | collective-permute-start | bytes 110600 | tf_op jit(solution)/shard_map/ppermute | solution.py:423
  9.3 4.9 %collective-permute-start.1 = (bf16[144,128]{1,0:T(8,128)(2,1)S(1)}, bf16[144,128]{1,0:T(8,128)(2,1)S(1)}, u32[]{:S(2)}, u32[]{:S(2)}) collective-permute-start(bf16[144,128]{1,0:T(8,128)(2,1)S(1)} %shard_map.181.refs_0_), channel_id=1, source_target_pairs={{0,8},{4,12},{8,0},{12,4},{1,9},{5,13},{9,1},{13,5},{2,10},{6,14},... | collective-permute-start | bytes 110600 | tf_op jit(solution)/shard_map/ppermute | solution.py:423
  9.3 4.9 %collective-permute-start = (bf16[144,128]{1,0:T(8,128)(2,1)S(1)}, bf16[144,128]{1,0:T(8,128)(2,1)S(1)}, u32[]{:S(2)}, u32[]{:S(2)}) collective-permute-start(bf16[144,128]{1,0:T(8,128)(2,1)S(1)} %shard_map.181.refs_0_), channel_id=1, source_target_pairs={{0,4},{4,0},{8,12},{12,8},{1,5},{5,1},{9,13},{13,9},{2,6},{6,2},{1... | collective-permute-start | bytes 110600 | tf_op jit(solution)/shard_map/ppermute | solution.py:423
  14.3 14.0 %copy-start.10 = (bf16[128,48]{1,0:T(8,128)(2,1)S(1)}, bf16[128,48]{1,0:T(8,128)(2,1)}, u32[]{:S(2)}) copy-start(bf16[128,48]{1,0:T(8,128)(2,1)} %constant.35.clone.ex) | copy-start | bytes 36868
  14.3 14.0 %copy-start.11 = (bf16[128,512]{1,0:T(8,128)(2,1)S(1)}, bf16[128,512]{1,0:T(8,128)(2,1)}, u32[]{:S(2)}) copy-start(bf16[128,512]{1,0:T(8,128)(2,1)} %constant.33.clone.ph) | copy-start | bytes 393220
  14.3 14.0 %copy-start.12 = (bf16[96,128]{1,0:T(8,128)(2,1)S(1)}, bf16[96,128]{1,0:T(8,128)(2,1)}, u32[]{:S(2)}) copy-start(bf16[96,128]{1,0:T(8,128)(2,1)} %constant.25.clone.fx) | copy-start | bytes 73732
  17.1 11.2 %copy-start.5 = (bf16[128,256]{1,0:T(8,128)(2,1)S(1)}, bf16[128,256]{1,0:T(8,128)(2,1)}, u32[]{:S(2)}) copy-start(bf16[128,256]{1,0:T(8,128)(2,1)} %constant.34.clone.gy) | copy-start | bytes 196612
  17.1 11.2 %copy-start.7 = (bf16[128,256]{1,0:T(8,128)(2,1)S(1)}, bf16[128,256]{1,0:T(8,128)(2,1)}, u32[]{:S(2)}) copy-start(bf16[128,256]{1,0:T(8,128)(2,1)} %constant.24.clone.fy) | copy-start | bytes 196612
  29.8 5.8 %collective-permute-start.6 = (bf16[128,128]{1,0:T(8,128)(2,1)S(1)}, bf16[128,128]{1,0:T(8,128)(2,1)S(1)}, u32[]{:S(2)}, u32[]{:S(2)}) collective-permute-start(bf16[128,128]{1,0:T(8,128)(2,1)S(1)} %get-tuple-element.9.refs_0_), channel_id=1, source_target_pairs={{0,12},{4,8},{8,4},{12,0},{1,13},{5,9},{9,5},{13,1},{2,14},{6,10},... | collective-permute-start | bytes 98312 | tf_op jit(solution)/shard_map/ppermute | solution.py:423
  30.4 5.2 %collective-permute-start.5 = (bf16[128,128]{1,0:T(8,128)(2,1)S(1)}, bf16[128,128]{1,0:T(8,128)(2,1)S(1)}, u32[]{:S(2)}, u32[]{:S(2)}) collective-permute-start(bf16[128,128]{1,0:T(8,128)(2,1)S(1)} %get-tuple-element.9.refs_0_), channel_id=1, source_target_pairs={{0,8},{4,12},{8,0},{12,4},{1,9},{5,13},{9,1},{13,5},{2,10},{6,14},... | collective-permute-start | bytes 98312 | tf_op jit(solution)/shard_map/ppermute | solution.py:423
  31.5 4.7 %collective-permute-start.4 = (bf16[128,128]{1,0:T(8,128)(2,1)S(1)}, bf16[128,128]{1,0:T(8,128)(2,1)S(1)}, u32[]{:S(2)}, u32[]{:S(2)}) collective-permute-start(bf16[128,128]{1,0:T(8,128)(2,1)S(1)} %get-tuple-element.9.refs_0_), channel_id=1, source_target_pairs={{0,4},{4,0},{8,12},{12,8},{1,5},{5,1},{9,13},{13,9},{2,6},{6,2},{1... | collective-permute-start | bytes 98312 | tf_op jit(solution)/shard_map/ppermute | solution.py:423

commit v3 on v2

--- a/solution.py
+++ b/solution.py
@@ -154,15 +154,14 @@
     return lax.broadcasted_iota(jnp.int32, shape, len(shape) - 1)
 
 
-def arrange_body(tabs, dose, kern, out):
+def arrange_body(tabs, kern, out):
     freq, mid, rows = tabs.freq, tabs.mid, tabs.rows
     number, tall = out.shape[0], up(freq, 8)
-    root = jnp.sqrt(jnp.full((1, 1), dose[0], F32))
     side = jnp.zeros((freq, HALF - freq), F32)
     below = jnp.zeros((tall - freq, LANES), F32)
     rights = []
     for k in range(number):
-        both = jnp.concatenate([kern[0, 0, k] * root, side, kern[1, 0, k] * root, side], axis=1)
+        both = jnp.concatenate([kern[0, 0, k], side, kern[1, 0, k], side], axis=1)
         rights.append(jnp.concatenate([both, below], axis=0))
     rights = jnp.concatenate(rights, axis=0).astype(BF)
     row = lax.broadcasted_iota(jnp.int32, (LANES, LANES), 0)
@@ -208,13 +207,16 @@
         out[c * sent : (c + 1) * sent] = pack(tabs, spec * scale - centre)
 
 
-def first_body(tabs, slots, owner, local, shift, theta, fy, fx, out):
+def first_body(tabs, slots, owner, local, shift, theta, fy, fx, out, table):
     spectra(tabs, slots, theta[...], fy, fx, out)
     base = theta.shape[0] * packing(tabs)[0]
     row = lax.broadcasted_iota(jnp.int32, (INFO, LANES), 0)
     col = lane_of((INFO, LANES))
     info = jnp.zeros((INFO, LANES), jnp.int32)
     for i in range(local.shape[0]):
+        table[0, i] = owner[i]
+        table[1, i] = local[i]
+        table[2, i] = shift[i]
         value = jnp.where(row == 0, owner[i], jnp.where(row == 1, local[i], shift[i]))
         info = jnp.where((col == i) & (row < 3), value, info)
     out[base : base + INFO] = info.astype(F32).astype(BF)
@@ -245,12 +247,12 @@
         out[pl.ds(place * tiles, tiles)] = part.reshape(tiles, cells, 2 * LANES)
 
 
-def tile_body(tabs, n, cells, tiles, copies, owner, local, shift, *refs):
+def tile_body(tabs, n, cells, tiles, copies, table, dose, *refs):
     payload, refs = refs[:n], refs[n:]
     arranged, refs = refs[:tiles], refs[tiles:]
     target, ph, gyy, gyy_t, gx, gx_t, w, w_t, out, held, wide, tall, near = refs
     rows, cell, grid = tabs.rows, tabs.cell, tabs.grid
-    slots = local.shape[0] // tiles
+    slots = table.shape[1] // tiles
     z, j = lax.axis_index("cells"), lax.axis_index("kern")
     for k in range(n):
         sent = packing(tabs)[0]
@@ -258,9 +260,9 @@
     spec = jnp.zeros((rows, LANES), F32)
     for s in range(slots):
         i = j * slots + s
-        which = source(n, z, owner[i]) * cells + local[i]
+        which = source(n, z, table[0, i]) * cells + table[1, i]
         one = unpack(tabs, held[which])
-        turn = ph[pl.ds(shift[i], 1)]
+        turn = ph[pl.ds(table[2, i], 1)]
         spec = spec + one * turn[:, :LANES] + swap(one) * turn[:, LANES:]
     left = lane_of((rows, LANES)) < HALF
     other = swap(spec)
@@ -295,8 +297,8 @@
     if w.shape[1] > 3 * grid:
         stack.append(jnp.zeros((w.shape[1] - 3 * grid, cell), F32))
     image = dot(w[...], jnp.concatenate(stack, axis=0).astype(BF))
-    resist = jax.nn.sigmoid(STEEP * (image - 1.0))
-    pressure = 4.0 * STEEP * (resist - wanted) * resist * (1.0 - resist)
+    resist = jax.nn.sigmoid(STEEP * (dose[0] * image - 1.0))
+    pressure = 4.0 * STEEP * dose[0] * (resist - wanted) * resist * (1.0 - resist)
     push = dot(w_t[...], pressure.astype(BF))
     for m in range(0, number, 2):
         pair = []
@@ -389,8 +391,10 @@
 SMEM = pl.BlockSpec(memory_space=pltpu.SMEM)
 
 
-def call(body, scalars, arrays, outs, scratch=(), far=(), out_far=False):
+def call(body, scalars, arrays, outs, scratch=(), name=None, far=(), out_far=False):
     many = isinstance(outs, list)
+    if name == "tile":
+        scalars = [pltpu.with_memory_space_constraint(array, pltpu.SMEM) for array in scalars]
     arrays = [
         array if place in far else pltpu.with_memory_space_constraint(array, pltpu.VMEM)
         for place, array in enumerate(arrays)
@@ -400,7 +404,9 @@
         body,
         out_shape=outs,
         in_specs=[SMEM] * len(scalars) + [VMEM] * len(arrays),
-        out_specs=[VMEM] * len(outs) if many else out_spec,
+        out_specs=[
+            SMEM if out.memory_space == pltpu.SMEM else VMEM for out in outs
+        ] if many else out_spec,
         scratch_shapes=list(scratch),
     )(*scalars, *arrays)
 
@@ -435,11 +441,15 @@
     inst_owner = inst_owner[:, 0]
     rows, sent = tabs.rows, packing(tabs)[0]
     band = cell // (n_kern * n_corners)
-    payload = call(
+    payload, table = call(
         functools.partial(first_body, tabs, slots),
         [inst_owner, inst_local, inst_shift],
         [theta, tabs.fy, tabs.fx],
-        shape((cells * sent + INFO, LANES), BF),
+        [
+            shape((cells * sent + INFO, LANES), BF),
+            pltpu.SMEM((3, inst_local.shape[0]), jnp.int32),
+        ],
+        name="first",
         far=(0, 1, 2),
     )
     payloads = [payload]
@@ -447,16 +457,19 @@
         payloads.append(shifted(payload, "cells", k))
     own = call(
         functools.partial(arrange_body, tabs),
-        [dose],
+        [],
         [kernels],
         shape((kernels.shape[2], 2 * rows, LANES), BF),
+        name="arrange",
     )
-    arranged = [own] + [shifted(own, "kern", k) for k in range(1, n_kern)]
+    arranged = [own]
+    for k in range(1, n_kern):
+        arranged.append(shifted(own, "kern", k))
     copies = n * n_corners * n_kern
     for iteration in range(ITERS):
         grads = call(
             functools.partial(tile_body, tabs, n, cells, tiles, copies),
-            [inst_owner, inst_local, inst_shift],
+            [table, dose],
             payloads
             + arranged
             + [target, tabs.ph, tabs.gyy, tabs.gyy_t, tabs.gx, tabs.gx_t, tabs.w, tabs.w_t],
@@ -467,6 +480,7 @@
                 pltpu.VMEM((n_kern * kernels.shape[2], 4 * rows, cell), BF),
                 pltpu.VMEM((n_kern * kernels.shape[2], 2 * tabs.grid, cell), F32),
             ],
+            name="tile",
         )
         grads = lax.all_to_all(grads, ("cells", "corners", "kern"), 0, 0, tiled=True)
         if iteration == ITERS - 1:
@@ -480,6 +494,7 @@
                     pltpu.VMEM((cells, band, cell), F32),
                     pltpu.SemaphoreType.DMA((cells,)),
                 ],
+                name="last",
                 out_far=True,
             )
         theta, sums, payload = call(
@@ -491,6 +506,7 @@
                 shape((n * tiles, cells, 2 * LANES), F32),
                 shape((cells * sent, LANES), BF),
             ],
+            name="update",
         )
         payloads = [payload]
         for k in range(1, n):

time: 50.9 us -> 48.7 us (0.957)
  Pallas kernels: 10.6 us -> 9.04 us
  waiting for transfers between devices: 6.11 us -> 5.46 us
    pallas_call x6, Pallas kernels: 10.6 us -> 9.04 us  [call(): pl.pallas_call(body, out_shape=outs, in_specs=[SMEM] * len(scalars) + [VM...]
    ppermute x7, waiting for transfers between devices: 6.11 us -> 5.46 us  [shifted(): return lax.ppermute(array, axis, moves)]
where the time goes in v3:
time: 48.7 us; the launch traced here: 48.4 us
  blocking collectives  21.6 us (44%)
  starting transfers between devices  10.3 us (21%)
  Pallas kernels  9.04 us (19%)
  waiting for transfers between devices  5.46 us (11%)
  local copies, waits for them, and re-layouts  1.13 us (2%)
  between operations  0.84 us (2%)
    all_to_all x2, blocking collectives, per_device(): lax.all_to_all(grads, ('cells', 'corners', 'kern'), 0, 0, tiled=True)  21.6 us
    ppermute x7, starting transfers between devices, shifted(): return lax.ppermute(array, axis, moves)  10.3 us
    pallas_call x6, Pallas kernels, call(): pl.pallas_call(body, out_shape=outs, in_specs=[SMEM] * len(scalars) + [VM...  9.04 us
    ppermute x7, waiting for transfers between devices, shifted(): return lax.ppermute(array, axis, moves)  5.46 us
    unnamed x29, local copies, waits for them, and re-layouts  1.13 us
  transfers between devices with their start and end apart: 7, of which 4 were waited for; matrix products, arithmetic and copies ran while one was open for 0% of the time, Pallas kernels for 4%

profile of v3, /device:TPU:0, one launch (start us, length us, event | category | flops | bytes accessed | tf_op | source)
XLA Modules:
  0.0 48.4 jit_solution(15068964162965339845)
XLA Ops:
  0.0 1.0 %copy.20.kern = f32[2,1,12,35,35]{4,3,2,1,0:T(8,128)S(1)} copy(f32[2,1,12,35,35]{4,1,3,2,0:T(1,128)} %param.21) | data formatting | bytes 235200 | tf_op args[2]
  1.0 0.0 copy-start.13
  1.1 0.4 shard_map.182.refs_4_
  1.4 0.6 %collective-permute-start.3 = (bf16[12,48,128]{2,1,0:T(8,128)(2,1)S(1)}, bf16[12,48,128]{2,1,0:T(8,128)(2,1)S(1)}, u32[]{:S(2)}, u32[]{:S(2)}) collective-permute-start(bf16[12,48,128]{2,1,0:T(8,128)(2,1)S(1)} %shard_map.182.refs_4_), channel_id=1, source_target_pairs={{0,1},{1,0},{2,3},{3,2},{4,5},{5,4},{6,7},{7,6},{8,9},{9,8},{10,11... | collective-permute-start | bytes 442376 | tf_op jit(solution)/shard_map/ppermute | solution.py:429
  2.0 0.0 copy-start.6
  2.0 0.0 copy-start.8
  2.0 0.0 copy-start.9
  2.1 1.9 %shard_map.181 = (bf16[144,128]{1,0:T(8,128)(2,1)S(1)}, s32[3,16]{1,0:T(4,128)S(4)}) custom-call(s32[16]{0:T(128)} %bitcast.1, s32[16]{0:T(128)} %local.1, s32[16]{0:T(128)} %shift.1, f32[8,128,128]{2,1,0:T(8,128)} %theta.3, bf16[128,256]{1,0:T(8,128)(2,1)} %constant.24.clone.fy, bf16[96,128]{1,0:T(8,128)(2,1)} %constant.25.clone.fx), custom_call_target="tpu_custom_call" | custom-call | tf_op jit(solution)/shard_map/pallas_call | solution.py:403
  3.9 4.7 %collective-permute-start.2 = (bf16[144,128]{1,0:T(8,128)(2,1)S(1)}, bf16[144,128]{1,0:T(8,128)(2,1)S(1)}, u32[]{:S(2)}, u32[]{:S(2)}) collective-permute-start(bf16[144,128]{1,0:T(8,128)(2,1)S(1)} %get-tuple-element.11.refs_0_), channel_id=1, source_target_pairs={{0,12},{4,8},{8,4},{12,0},{1,13},{5,9},{9,5},{13,1},{2,14},{6,10},... | collective-permute-start | bytes 110600 | tf_op jit(solution)/shard_map/ppermute | solution.py:429
  8.6 0.0 collective-permute-start.1
  8.6 0.6 %collective-permute-start = (bf16[144,128]{1,0:T(8,128)(2,1)S(1)}, bf16[144,128]{1,0:T(8,128)(2,1)S(1)}, u32[]{:S(2)}, u32[]{:S(2)}) collective-permute-start(bf16[144,128]{1,0:T(8,128)(2,1)S(1)} %get-tuple-element.11.refs_0_), channel_id=1, source_target_pairs={{0,4},{4,0},{8,12},{12,8},{1,5},{5,1},{9,13},{13,9},{2,6},{6,2},{1... | collective-permute-start | bytes 110600 | tf_op jit(solution)/shard_map/ppermute | solution.py:429
  9.9 0.9 %collective-permute-done.2.refs_3_ = bf16[144,128]{1,0:T(8,128)(2,1)S(1)} collective-permute-done((bf16[144,128]{1,0:T(8,128)(2,1)S(1)}, bf16[144,128]{1,0:T(8,128)(2,1)S(1)}, u32[]{:S(2)}, u32[]{:S(2)}) %collective-permute-start.2) | collective-permute-done | bytes 36896 | tf_op jit(solution)/shard_map/ppermute | solution.py:429
  10.8 2.7 %collective-permute-done.1.refs_2_ = bf16[144,128]{1,0:T(8,128)(2,1)S(1)} collective-permute-done((bf16[144,128]{1,0:T(8,128)(2,1)S(1)}, bf16[144,128]{1,0:T(8,128)(2,1)S(1)}, u32[]{:S(2)}, u32[]{:S(2)}) %collective-permute-start.1) | collective-permute-done | bytes 36896 | tf_op jit(solution)/shard_map/ppermute | solution.py:429
  13.5 0.0 collective-permute-done.refs_1_
  13.5 0.0 collective-permute-done.3.refs_5_
  13.6 0.0 copy-start
  13.6 0.0 copy-start.10
  13.6 0.0 copy-start.11
  13.6 0.0 copy-start.12
  13.6 2.0 %shard_map.183 = bf16[16,16,128]{2,1,0:T(8,128)(2,1)S(1)} custom-call(s32[3,16]{1,0:T(4,128)S(4)} %get-tuple-element.10.table, f32[1]{0:T(128)S(6)} %copy.21.dose, bf16[144,128]{1,0:T(8,128)(2,1)S(1)} %get-tuple-element.11.refs_0_, bf16[144,128]{1,0:T(8,128)(2,1)S(1)} %collective-permute-done.refs_1_, bf16[144,128]{1,0:T(8,128)(2,1)S(1)} %collective-permute-done.1.refs_2_, ...), custom_call_target="tpu_custom_call" | custom-call | tf_op jit(solution)/shard_map/pallas_call | solution.py:403
  15.6 0.0 copy-start.5
  15.6 0.0 copy-start.7
  15.6 11.2 %all_to_all.10.grads = bf16[16,16,128]{2,1,0:T(8,128)(2,1)S(1)} all-to-all(bf16[16,16,128]{2,1,0:T(8,128)(2,1)S(1)} %shard_map.183), channel_id=1, replica_groups=mesh['groups'=2,'cells'=4,'corners'=2,'kern'=2] {'cells','corners','kern'}, dimensions={0} | all-to-all | bytes 131072 | tf_op jit(solution)/shard_map/all_to_all | solution.py:485
  26.8 1.5 %shard_map.184 = (f32[8,128,128]{2,1,0:T(8,128)S(1)}, f32[8,8,256]{2,1,0:T(8,128)S(1)}, bf16[128,128]{1,0:T(8,128)(2,1)S(1)}) custom-call(f32[8,128,128]{2,1,0:T(8,128)S(1)} %copy-done, bf16[16,16,128]{2,1,0:T(8,128)(2,1)S(1)} %all_to_all.10.grads, bf16[128,512]{1,0:T(8,128)(2,1)S(1)} %copy-done.11, bf16[128,256]{1,0:T(8,128)(2,1)S(1)} %copy-done.5, ...), custom_call_target="tpu_custom_call" | custom-call | tf_op jit(solution)/shard_map/pallas_call | solution.py:403
  28.3 0.6 %collective-permute-start.6 = (bf16[128,128]{1,0:T(8,128)(2,1)S(1)}, bf16[128,128]{1,0:T(8,128)(2,1)S(1)}, u32[]{:S(2)}, u32[]{:S(2)}) collective-permute-start(bf16[128,128]{1,0:T(8,128)(2,1)S(1)} %get-tuple-element.13.refs_0_), channel_id=1, source_target_pairs={{0,12},{4,8},{8,4},{12,0},{1,13},{5,9},{9,5},{13,1},{2,14},{6,10},... | collective-permute-start | bytes 98312 | tf_op jit(solution)/shard_map/ppermute | solution.py:429
  28.9 1.0 %collective-permute-start.5 = (bf16[128,128]{1,0:T(8,128)(2,1)S(1)}, bf16[128,128]{1,0:T(8,128)(2,1)S(1)}, u32[]{:S(2)}, u32[]{:S(2)}) collective-permute-start(bf16[128,128]{1,0:T(8,128)(2,1)S(1)} %get-tuple-element.13.refs_0_), channel_id=1, source_target_pairs={{0,8},{4,12},{8,0},{12,4},{1,9},{5,13},{9,1},{13,5},{2,10},{6,14},... | collective-permute-start | bytes 98312 | tf_op jit(solution)/shard_map/ppermute | solution.py:429
  29.9 2.8 %collective-permute-start.4 = (bf16[128,128]{1,0:T(8,128)(2,1)S(1)}, bf16[128,128]{1,0:T(8,128)(2,1)S(1)}, u32[]{:S(2)}, u32[]{:S(2)}) collective-permute-start(bf16[128,128]{1,0:T(8,128)(2,1)S(1)} %get-tuple-element.13.refs_0_), channel_id=1, source_target_pairs={{0,4},{4,0},{8,12},{12,8},{1,5},{5,1},{9,13},{13,9},{2,6},{6,2},{1... | collective-permute-start | bytes 98312 | tf_op jit(solution)/shard_map/ppermute | solution.py:429
  32.7 1.4 %collective-permute-done.6.refs_3_ = bf16[128,128]{1,0:T(8,128)(2,1)S(1)} collective-permute-done((bf16[128,128]{1,0:T(8,128)(2,1)S(1)}, bf16[128,128]{1,0:T(8,128)(2,1)S(1)}, u32[]{:S(2)}, u32[]{:S(2)}) %collective-permute-start.6) | collective-permute-done | bytes 32800 | tf_op jit(solution)/shard_map/ppermute | solution.py:429
  34.1 0.5 %collective-permute-done.4.refs_1_ = bf16[128,128]{1,0:T(8,128)(2,1)S(1)} collective-permute-done((bf16[128,128]{1,0:T(8,128)(2,1)S(1)}, bf16[128,128]{1,0:T(8,128)(2,1)S(1)}, u32[]{:S(2)}, u32[]{:S(2)}) %collective-permute-start.4) | collective-permute-done | bytes 32800 | tf_op jit(solution)/shard_map/ppermute | solution.py:429
  34.6 2.0 %shard_map.185 = bf16[16,16,128]{2,1,0:T(8,128)(2,1)S(1)} custom-call(s32[3,16]{1,0:T(4,128)S(4)} %get-tuple-element.10.table, f32[1]{0:T(128)S(6)} %copy.21.dose, bf16[128,128]{1,0:T(8,128)(2,1)S(1)} %get-tuple-element.13.refs_0_, bf16[128,128]{1,0:T(8,128)(2,1)S(1)} %collective-permute-done.4.refs_1_, bf16[128,128]{1,0:T(8,128)(2,1)S(1)} %collective-permute-done.5.refs_2_, ...), custom_call_target="tpu_custom_call" | custom-call | tf_op jit(solution)/shard_map/pallas_call | solution.py:403
  36.6 10.4 %all_to_all.11.grads = bf16[16,16,128]{2,1,0:T(8,128)(2,1)S(1)} all-to-all(bf16[16,16,128]{2,1,0:T(8,128)(2,1)S(1)} %shard_map.185), channel_id=1, replica_groups=mesh['groups'=2,'cells'=4,'corners'=2,'kern'=2] {'cells','corners','kern'}, dimensions={0} | all-to-all | bytes 131072 | tf_op jit(solution)/shard_map/all_to_all | solution.py:485
  47.0 1.3 %shard_map.186 = f32[8,32,128]{2,1,0:T(8,128)} custom-call(f32[8,128,128]{2,1,0:T(8,128)S(1)} %get-tuple-element.12.theta, bf16[16,16,128]{2,1,0:T(8,128)(2,1)S(1)} %all_to_all.11.grads, f32[8,8,256]{2,1,0:T(8,128)S(1)} %get-tuple-element.14.sums, bf16[128,256]{1,0:T(8,128)(2,1)S(1)} %copy-done.5, bf16[128,48]{1,0:T(8,128)(2,1)S(1)} %copy-done.10), custom_call_target="tpu_custom_call" | custom-call | tf_op jit(solution)/shard_map/pallas_call | solution.py:403
  (19 shorter events, 0.0 us)
Async XLA Ops:
  1.0 12.4 %copy-start.13 = (bf16[72,128]{1,0:T(8,128)(2,1)S(1)}, bf16[72,128]{1,0:T(8,128)(2,1)}, u32[]{:S(2)}) copy-start(bf16[72,128]{1,0:T(8,128)(2,1)} %constant.32.clone.refs_13_) | copy-start | bytes 55300
  1.4 12.0 %collective-permute-start.3 = (bf16[12,48,128]{2,1,0:T(8,128)(2,1)S(1)}, bf16[12,48,128]{2,1,0:T(8,128)(2,1)S(1)}, u32[]{:S(2)}, u32[]{:S(2)}) collective-permute-start(bf16[12,48,128]{2,1,0:T(8,128)(2,1)S(1)} %shard_map.182.refs_4_), channel_id=1, source_target_pairs={{0,1},{1,0},{2,3},{3,2},{4,5},{5,4},{6,7},{7,6},{8,9},{9,8},{10,11... | collective-permute-start | bytes 442376 | tf_op jit(solution)/shard_map/ppermute | solution.py:429
  2.0 11.5 %copy-start.1 = (bf16[256,256]{1,0:T(8,128)(2,1)S(1)}, bf16[256,256]{1,0:T(8,128)(2,1)}, u32[]{:S(2)}) copy-start(bf16[256,256]{1,0:T(8,128)(2,1)} %constant.28.clone.refs_9_) | copy-start | bytes 393220
  2.0 11.5 %copy-start.2 = (bf16[256,256]{1,0:T(8,128)(2,1)S(1)}, bf16[256,256]{1,0:T(8,128)(2,1)}, u32[]{:S(2)}) copy-start(bf16[256,256]{1,0:T(8,128)(2,1)} %constant.27.clone.refs_8_) | copy-start | bytes 393220
  2.0 11.5 %copy-start.3 = (f32[128,256]{1,0:T(8,128)S(1)}, f32[128,256]{1,0:T(8,128)}, u32[]{:S(2)}) copy-start(f32[128,256]{1,0:T(8,128)} %constant.26.clone.refs_7_) | copy-start | bytes 393220
  2.0 11.5 %copy-start.4 = (bf16[2,128,128]{2,1,0:T(8,128)(2,1)S(1)}, bf16[2,128,128]{2,1,0:T(8,128)(2,1)}, u32[]{:S(2)}) copy-start(bf16[2,128,128]{2,1,0:T(8,128)(2,1)} %refs_6_.3) | copy-start | bytes 196612
  2.0 11.5 %copy-start.6 = (bf16[128,224]{1,0:T(8,128)(2,1)S(1)}, bf16[128,224]{1,0:T(8,128)(2,1)}, u32[]{:S(2)}) copy-start(bf16[128,224]{1,0:T(8,128)(2,1)} %constant.31.clone.refs_12_) | copy-start | bytes 172036
  2.0 11.5 %copy-start.8 = (bf16[96,144]{1,0:T(8,128)(2,1)S(1)}, bf16[96,144]{1,0:T(8,128)(2,1)}, u32[]{:S(2)}) copy-start(bf16[96,144]{1,0:T(8,128)(2,1)} %constant.30.clone.refs_11_) | copy-start | bytes 82948
  2.0 11.5 %copy-start.9 = (bf16[144,96]{1,0:T(8,128)(2,1)S(1)}, bf16[144,96]{1,0:T(8,128)(2,1)}, u32[]{:S(2)}) copy-start(bf16[144,96]{1,0:T(8,128)(2,1)} %constant.29.clone.refs_10_) | copy-start | bytes 82948
  3.9 6.9 %collective-permute-start.2 = (bf16[144,128]{1,0:T(8,128)(2,1)S(1)}, bf16[144,128]{1,0:T(8,128)(2,1)S(1)}, u32[]{:S(2)}, u32[]{:S(2)}) collective-permute-start(bf16[144,128]{1,0:T(8,128)(2,1)S(1)} %get-tuple-element.11.refs_0_), channel_id=1, source_target_pairs={{0,12},{4,8},{8,4},{12,0},{1,13},{5,9},{9,5},{13,1},{2,14},{6,10},... | collective-permute-start | bytes 110600 | tf_op jit(solution)/shard_map/ppermute | solution.py:429
  8.6 4.9 %collective-permute-start.1 = (bf16[144,128]{1,0:T(8,128)(2,1)S(1)}, bf16[144,128]{1,0:T(8,128)(2,1)S(1)}, u32[]{:S(2)}, u32[]{:S(2)}) collective-permute-start(bf16[144,128]{1,0:T(8,128)(2,1)S(1)} %get-tuple-element.11.refs_0_), channel_id=1, source_target_pairs={{0,8},{4,12},{8,0},{12,4},{1,9},{5,13},{9,1},{13,5},{2,10},{6,14},... | collective-permute-start | bytes 110600 | tf_op jit(solution)/shard_map/ppermute | solution.py:429
  8.6 4.9 %collective-permute-start = (bf16[144,128]{1,0:T(8,128)(2,1)S(1)}, bf16[144,128]{1,0:T(8,128)(2,1)S(1)}, u32[]{:S(2)}, u32[]{:S(2)}) collective-permute-start(bf16[144,128]{1,0:T(8,128)(2,1)S(1)} %get-tuple-element.11.refs_0_), channel_id=1, source_target_pairs={{0,4},{4,0},{8,12},{12,8},{1,5},{5,1},{9,13},{13,9},{2,6},{6,2},{1... | collective-permute-start | bytes 110600 | tf_op jit(solution)/shard_map/ppermute | solution.py:429
  13.6 13.2 %copy-start = (f32[8,128,128]{2,1,0:T(8,128)S(1)}, f32[8,128,128]{2,1,0:T(8,128)}, u32[]{:S(2)}) copy-start(f32[8,128,128]{2,1,0:T(8,128)} %theta.3) | copy-start | bytes 1572868
  13.6 13.2 %copy-start.10 = (bf16[128,48]{1,0:T(8,128)(2,1)S(1)}, bf16[128,48]{1,0:T(8,128)(2,1)}, u32[]{:S(2)}) copy-start(bf16[128,48]{1,0:T(8,128)(2,1)} %constant.35.clone.ex) | copy-start | bytes 36868
  13.6 13.2 %copy-start.11 = (bf16[128,512]{1,0:T(8,128)(2,1)S(1)}, bf16[128,512]{1,0:T(8,128)(2,1)}, u32[]{:S(2)}) copy-start(bf16[128,512]{1,0:T(8,128)(2,1)} %constant.33.clone.ph) | copy-start | bytes 393220
  13.6 13.2 %copy-start.12 = (bf16[96,128]{1,0:T(8,128)(2,1)S(1)}, bf16[96,128]{1,0:T(8,128)(2,1)}, u32[]{:S(2)}) copy-start(bf16[96,128]{1,0:T(8,128)(2,1)} %constant.25.clone.fx) | copy-start | bytes 73732
  15.6 11.2 %copy-start.5 = (bf16[128,256]{1,0:T(8,128)(2,1)S(1)}, bf16[128,256]{1,0:T(8,128)(2,1)}, u32[]{:S(2)}) copy-start(bf16[128,256]{1,0:T(8,128)(2,1)} %constant.34.clone.gy) | copy-start | bytes 196612
  15.6 11.2 %copy-start.7 = (bf16[128,256]{1,0:T(8,128)(2,1)S(1)}, bf16[128,256]{1,0:T(8,128)(2,1)}, u32[]{:S(2)}) copy-start(bf16[128,256]{1,0:T(8,128)(2,1)} %constant.24.clone.fy) | copy-start | bytes 196612
  28.3 5.8 %collective-permute-start.6 = (bf16[128,128]{1,0:T(8,128)(2,1)S(1)}, bf16[128,128]{1,0:T(8,128)(2,1)S(1)}, u32[]{:S(2)}, u32[]{:S(2)}) collective-permute-start(bf16[128,128]{1,0:T(8,128)(2,1)S(1)} %get-tuple-element.13.refs_0_), channel_id=1, source_target_pairs={{0,12},{4,8},{8,4},{12,0},{1,13},{5,9},{9,5},{13,1},{2,14},{6,10},... | collective-permute-start | bytes 98312 | tf_op jit(solution)/shard_map/ppermute | solution.py:429
  28.9 5.2 %collective-permute-start.5 = (bf16[128,128]{1,0:T(8,128)(2,1)S(1)}, bf16[128,128]{1,0:T(8,128)(2,1)S(1)}, u32[]{:S(2)}, u32[]{:S(2)}) collective-permute-start(bf16[128,128]{1,0:T(8,128)(2,1)S(1)} %get-tuple-element.13.refs_0_), channel_id=1, source_target_pairs={{0,8},{4,12},{8,0},{12,4},{1,9},{5,13},{9,1},{13,5},{2,10},{6,14},... | collective-permute-start | bytes 98312 | tf_op jit(solution)/shard_map/ppermute | solution.py:429
  29.9 4.7 %collective-permute-start.4 = (bf16[128,128]{1,0:T(8,128)(2,1)S(1)}, bf16[128,128]{1,0:T(8,128)(2,1)S(1)}, u32[]{:S(2)}, u32[]{:S(2)}) collective-permute-start(bf16[128,128]{1,0:T(8,128)(2,1)S(1)} %get-tuple-element.13.refs_0_), channel_id=1, source_target_pairs={{0,4},{4,0},{8,12},{12,8},{1,5},{5,1},{9,13},{13,9},{2,6},{6,2},{1... | collective-permute-start | bytes 98312 | tf_op jit(solution)/shard_map/ppermute | solution.py:429
